TPU v7x, 512 devices: a whole 4x4x16 slice. The times are simulated.
512 devices in a mesh: ax: 32 (over x_lo, z), az: 16 (over y, x_hi, core).
Axes of the slice: x: 4 (x_hi: 2, x_lo: 2; x = x_hi * 2 + x_lo), y: 4, z: 16, core: 2. Of those that a mesh axis runs over, the one named last changes fastest.
Arguments:
- conserved: float32 [5, 256, 1024, 128], P(None, 'ax', 'az'), may hold values from -0.6 to 3, as said below
- panel_cells: int32 [262144], P(('ax', 'az')), may hold values from 0 to 65535
- panel_counts: int32 [512], P(('ax', 'az')), may hold values from 1 to 512, 131072 in all
- time_bins: int32 [262144, 64], P(('ax', 'az')), may hold values from 0 to 1023
- amplitudes: float32 [262144, 64], P(('ax', 'az')), may hold values from 0.5 to 2
Outputs:
- section: float32 [5, 256, 1024, 128], P(None, 'ax', 'az')
- signal: float32 [64, 1024], P(None, ('ax', 'az'))
Inputs may be any that keep to these rules, and one draw needn't show every extreme that they name: `conserved`: component 0 lies in 0.7 to 1.3, components 1 to 3 in -0.6 to 0.6, component 4 in 2.0 to 3.0. `panel_counts`: some device has exactly 512 live panel slots, each device at least one.
All inputs are finite; a program needn't handle non-finite values.
Results may differ from a plain program's by a relative error of at most 0.000076.
Values sent between devices are 32-bit elements; how exact they have to be, the bound alone decides.
A program may use at most 64 MiB of HBM per device.

v0:
```python
import math

import jax
import jax.numpy as jnp
from jax import lax
from jax.sharding import PartitionSpec as P

AZIMUTH = 1024
CYCLES = 8
OBSERVERS = 64
BINS = 1024


gas_factor = 0.4
time_step = 0.02
ref_pressure = 0.95


def padded_2(value, sides, width, wrap):
    for axis, dim in sides:
        size, length = (lax.axis_size(axis), value.shape[dim])
        up = [(i, (i + 1) % size) for i in range(size if wrap else size - 1)]
        down = [(j, i) for i, j in up]
        last = lax.slice_in_dim(value, length - width, length, axis=dim)
        leading = lax.slice_in_dim(value, 0, width, axis=dim)
        before = lax.ppermute(last, axis, up)
        after = lax.ppermute(leading, axis, down)
        value = jnp.concatenate([before, value, after], axis=dim)
    return value


def primitives(conserved):
    fluid_rho_value = conserved[0]
    axial_vel = conserved[1] / fluid_rho_value
    radial_vel = conserved[2] / fluid_rho_value
    swirl_vel = conserved[3] / fluid_rho_value
    kinetic = 0.5 * (
        conserved[1] * axial_vel + conserved[2] * radial_vel + conserved[3] * swirl_vel
    )
    thermo_stress_level = gas_factor * (conserved[4] - kinetic)
    return jnp.stack([fluid_rho_value, axial_vel, radial_vel, swirl_vel, thermo_stress_level])


def flux_along(primitive, stream_heading):
    fluid_rho_value = primitive[0]
    thermo_stress_level = primitive[4]
    stream_speed = [primitive[1], primitive[2], primitive[3]]
    overall_heat_work = thermo_stress_level / gas_factor + 0.5 * fluid_rho_value * (
        stream_speed[0] * stream_speed[0]
        + stream_speed[1] * stream_speed[1]
        + stream_speed[2] * stream_speed[2]
    )
    holder_buffer = stream_speed[stream_heading]
    divided_pieces = [fluid_rho_value * holder_buffer]
    for entry_number in range(3):
        forcing_contribution = fluid_rho_value * stream_speed[entry_number] * holder_buffer
        if entry_number == stream_heading:
            forcing_contribution = forcing_contribution + thermo_stress_level
        divided_pieces.append(forcing_contribution)
    divided_pieces.append((overall_heat_work + thermo_stress_level) * holder_buffer)
    return jnp.stack(divided_pieces)


def fourth_diff(padded, along_axis, length):
    near_diff = lax.slice_in_dim(padded, 3, length + 3, axis=along_axis) - lax.slice_in_dim(
        padded, 1, length + 1, axis=along_axis
    )
    far_diff = lax.slice_in_dim(padded, 4, length + 4, axis=along_axis) - lax.slice_in_dim(
        padded, 0, length, axis=along_axis
    )
    return (8.0 * near_diff - far_diff) / 12.0


def cycle_weights(length):
    modes = jnp.arange(length // 2 + 1).astype(jnp.float32)
    cutoff = 4.0 * (jnp.arange(CYCLES).astype(jnp.float32) + 1.0)
    return jnp.exp(-((modes[None, :] / cutoff[:, None]) ** 8))


def apply_filter(line_block, cycle_index, length):
    half = length // 2 + 1
    sample = jnp.arange(length)
    modes = jnp.arange(half)
    phase = (sample[:, None] * modes[None, :] % length).astype(jnp.float32) * (
        2.0 * math.pi / length
    )
    cos_table = jnp.cos(phase)
    sin_table = jnp.sin(phase)
    factor = jnp.where((modes == 0) | (modes == length // 2), 1.0, 2.0) / length
    selector = (cycle_index[:, None] == jnp.arange(CYCLES)[None, :]).astype(jnp.float32)
    line_weight = (
        jnp.dot(selector, cycle_weights(length), precision=lax.Precision.HIGHEST) * factor[None, :]
    )
    real_part = jnp.einsum("fln,nm->flm", line_block, cos_table, precision=lax.Precision.HIGHEST)
    imag_part = jnp.einsum("fln,nm->flm", line_block, sin_table, precision=lax.Precision.HIGHEST)
    smooth = jnp.einsum(
        "flm,nm->fln", real_part * line_weight[None], cos_table, precision=lax.Precision.HIGHEST
    )
    smooth = smooth + jnp.einsum(
        "flm,nm->fln", imag_part * line_weight[None], sin_table, precision=lax.Precision.HIGHEST
    )
    return smooth


def on_device(conserved, panel_cells, panel_counts, time_bins, amplitudes):
    planes_dev = conserved.shape[1]
    sector = conserved.shape[2]
    radial_all = conserved.shape[3]
    primitive = primitives(conserved)
    radius = jnp.arange(radial_all).astype(jnp.float32) + 0.5
    dtheta = 2.0 * math.pi / AZIMUTH
    axial_flux = flux_along(primitive, 0)
    swirl_flux = flux_along(primitive, 2)
    padded_x = padded_2(axial_flux, (("ax", 1),), 2, False)
    padded_t = padded_2(swirl_flux, (("az", 2),), 2, True)
    radial_flux = flux_along(primitive, 1)
    padded_r = jnp.pad(radial_flux * radius, ((0, 0), (0, 0), (0, 0), (2, 2)))
    tendency = -fourth_diff(padded_x, 1, planes_dev)
    tendency = tendency - fourth_diff(padded_r, 3, radial_all) / radius
    tendency = tendency - fourth_diff(padded_t, 2, sector) / (radius * dtheta)
    fluid_rho_value = primitive[0]
    radial_vel = primitive[2]
    swirl_vel = primitive[3]
    thermo_stress_level = primitive[4]
    zeros_field = jnp.zeros_like(fluid_rho_value)
    source = jnp.stack(
        [
            zeros_field,
            zeros_field,
            (thermo_stress_level + fluid_rho_value * swirl_vel * swirl_vel) / radius,
            -fluid_rho_value * radial_vel * swirl_vel / radius,
            zeros_field,
        ]
    )
    raw_section = conserved + time_step * (tendency + source)
    inner = raw_section[..., :CYCLES]
    lines = jnp.transpose(inner, (0, 1, 3, 2)).reshape(5, planes_dev * CYCLES, sector)
    line_block = lax.all_to_all(lines, "az", split_axis=1, concat_axis=2, tiled=True)
    line_count = line_block.shape[1]
    cycle_index = (lax.axis_index("az") * line_count + jnp.arange(line_count)) % CYCLES
    smooth = apply_filter(line_block, cycle_index, AZIMUTH)
    filtered = lax.all_to_all(smooth, "az", split_axis=2, concat_axis=1, tiled=True)
    filtered = jnp.transpose(filtered.reshape(5, planes_dev, CYCLES, sector), (0, 1, 3, 2))
    section = jnp.concatenate([filtered, raw_section[..., CYCLES:]], axis=3)
    slot_count = panel_cells.shape[0]
    live = jnp.arange(slot_count) < panel_counts[0]
    sampled = jnp.where(live, thermo_stress_level.reshape(-1)[panel_cells] - ref_pressure, 0.0)
    contrib = sampled[:, None] * amplitudes
    segment = jnp.arange(OBSERVERS)[None, :] * BINS + time_bins
    partial_signal = jax.ops.segment_sum(
        contrib.reshape(-1), segment.reshape(-1), num_segments=OBSERVERS * BINS
    )
    signal = lax.psum_scatter(
        partial_signal.reshape(OBSERVERS, BINS), ("ax", "az"), scatter_dimension=1, tiled=True
    )
    return (section, signal)


def solution(mesh):
    placed = (
        P(None, "ax", "az", None),
        P(("ax", "az")),
        P(("ax", "az")),
        P(("ax", "az"), None),
        P(("ax", "az"), None),
    )
    return jax.shard_map(
        on_device,
        mesh=mesh,
        in_specs=placed,
        out_specs=(P(None, "ax", "az", None), P(None, ("ax", "az"))),
        check_vma=False,
    )
```

profile of v0, /device:TPU:1, one launch (start us, length us, event | category | flops | bytes accessed | tf_op | source)
XLA Modules:
  0.0 676.1 jit_solution(17818139211325658250)
XLA Ops:
  7.2 1.8 constant_dynamic-update-slice_fusion
  9.0 0.7 compare_select_fusion
  10.4 2.2 add_dynamic-update-slice_fusion.1
  12.6 1.0 fusion.89
  13.6 0.1 fusion.58
  13.7 3.1 gather_fusion
  16.9 0.1 copy.84
  17.0 0.1 reshape.99
  17.2 0.1 broadcast_add_fusion
  17.3 0.1 copy.83
  17.4 0.1 reshape.97
  17.5 171.1 %scatter_custom_fusion = f32[65536]{0:T(1024)S(1)} fusion(s32[32768]{0:T(1024)S(1)} %reshape.97, f32[32768]{0:T(1024)S(1)} %reshape.99, f32[]{:T(128)} %constant.31.clone.1), kind=kCustom, calls=%fused_computation.96 | custom fusion | flops 32768 | bytes 262148 | tf_op jit(solution)/shard_map/scatter-add | solution.py:150
  188.6 0.7 reshape.86
  189.4 0.8 multiply_dynamic-update-slice_fusion.5
  190.2 0.6 copy-done.1
  190.9 0.9 multiply_dynamic-update-slice_fusion.7
  191.8 1.0 multiply_dynamic-update-slice_fusion.4
  192.8 0.8 multiply_dynamic-update-slice_fusion.3
  193.6 1.1 copy-done.2
  194.7 8.7 %collective-permute-start.2 = (f32[5,8,2,128]{3,1,2,0:T(8,128)S(1)}, f32[5,8,2,128]{3,1,2,0:T(8,128)S(1)}, u32[]{:S(2)}, u32[]{:S(2)}) collective-permute-start(f32[5,8,2,128]{3,1,2,0:T(8,128)S(1)} %copy.70), channel_id=1, source_target_pairs={{1,0},{2,1},{3,2},{4,3},{5,4},{6,5},{7,6},{8,7},{9,8},{10,9},{11,1... | collective-permute-start | bytes 122888 | tf_op jit(solution)/shard_map/ppermute | solution.py:27
  203.5 0.6 copy.72
  204.1 1.9 collective-permute-start.3
  206.0 2.0 fusion.90
  208.0 1.3 collective-permute-start
  209.3 4.7 collective-permute-start.1
  214.0 0.6 broadcast_multiply_fusion.2
  214.6 0.6 iota_convert_fusion
  215.2 0.6 select_multiply_fusion
  215.8 0.6 add_multiply_fusion
  216.4 0.9 broadcast_multiply_fusion
  217.2 0.6 and_select_fusion
  217.8 0.1 pad.10.clone
  217.9 0.8 copy.73
  218.7 0.4 collective-permute-done
  219.1 0.8 collective-permute-done.1
  220.0 4.0 multiply_add_fusion
  224.0 0.1 slice_bitcast_fusion
  224.1 0.6 copy.86
  224.7 0.8 reshape.112
  225.5 5.5 all-to-all-start
  231.0 0.2 convolution_multiply_fusion
  231.3 7.1 %all-to-all-done = f32[16,1,1280]{2,1,0:T(1,128)S(1)} async-done(((f32[16,1,1280]{2,1,0:T(1,128)}), f32[16,1,1280]{2,1,0:T(1,128)S(1)}, u32[]{:S(2)}, u32[]{:S(2)}) %all-to-all-start) | async-done | bytes 81952 | tf_op jit(solution)/shard_map/all_to_all | solution.py:138
  238.3 0.5 broadcast.212
  238.9 0.8 reduce
  239.7 0.1 reshape.113
  239.8 0.1 copy.94
  239.9 0.1 all_to_all.27
  240.0 10.2 %fusion.45 = f32[5,4,513]{2,0,1:T(8,128)S(1)} fusion(f32[5,4,1024]{2,1,0:T(4,128)S(1)} %all_to_all.27, f32[4,513]{1,0:T(4,128)S(1)} %convolution_multiply_fusion), kind=kOutput, calls=%fused_computation.65 | convolution fusion | flops 133439504 | bytes 131168 | tf_op jit(solution)/shard_map/fln,nm->flm/dot_general | solution.py:95
  250.2 10.1 %fusion.42 = f32[5,4,513]{2,0,1:T(8,128)S(1)} fusion(f32[5,4,1024]{2,1,0:T(4,128)S(1)} %all_to_all.27, f32[4,513]{1,0:T(4,128)S(1)} %convolution_multiply_fusion), kind=kOutput, calls=%fused_computation.64 | convolution fusion | flops 133439504 | bytes 131168 | tf_op jit(solution)/shard_map/fln,nm->flm/dot_general | solution.py:94
  260.3 9.7 %fusion.3 = f32[5,4,1024]{2,0,1:T(8,128)S(1)} fusion(f32[5,4,513]{2,0,1:T(8,128)S(1)} %fusion.45), kind=kOutput, calls=%fused_computation.12 | convolution fusion | flops 133429248 | bytes 122960 | tf_op jit(solution)/shard_map/flm,nm->fln/dot_general | solution.py:99
  269.9 9.6 %fusion.39 = f32[5,4,1024]{2,0,1:T(8,128)S(1)} fusion(f32[5,4,1024]{2,0,1:T(8,128)S(1)} %fusion.3, f32[5,4,513]{2,0,1:T(8,128)S(1)} %fusion.42), kind=kOutput, calls=%fused_computation.63 | convolution fusion | flops 133449728 | bytes 204880 | tf_op jit(solution)/shard_map/flm,nm->fln/dot_general | solution.py:96
  279.6 1.8 copy.79
  281.3 4.4 reshape.114
  285.7 3.8 all-to-all-start.1
  289.5 370.0 %all-reduce.4.cloned.1.call-done = f32[64,1024]{1,0:T(8,128)} async-done(((f32[64,1024]{1,0:T(8,128)}), f32[64,1024]{1,0:T(8,128)}) %all-reduce.4.cloned.1.call-update) | async-done | bytes 262160
  659.5 0.8 constant_dynamic-slice_fusion
  660.4 0.6 copy.85
  661.0 0.4 slice.118
  661.4 0.8 reduce.1
  662.2 2.6 reshape.115
  664.8 1.6 copy.87
  666.4 1.0 copy.81
  667.4 0.4 copy.82
  667.8 1.5 pad_maximum_fusion.4
  (42 shorter events, 0.3 us)
Async XLA Ops:
  7.2 652.4 %all-reduce.4.cloned.1.call-start = ((), (), s32[]{:S(2)}) async-start(), calls=%async_computation.2 | async-start | bytes 524288
  10.4 2.2 copy-start
  13.7 3.2 copy-start.5
  13.7 3.4 copy-start.6
  189.4 1.5 copy-start.1
  189.4 4.2 copy-start.7
  193.6 1.1 copy-start.2
  193.6 22.7 %copy-start.4 = (f32[5,8,64,128]{3,2,1,0:T(8,128)S(1)}, f32[5,8,64,128]{3,2,1,0:T(8,128)}, u32[]{:S(2)}) copy-start(f32[5,8,64,128]{3,2,1,0:T(8,128)} %get-tuple-element.40) | copy-start | bytes 3932164
  194.7 23.2 %collective-permute-start.2 = (f32[5,8,2,128]{3,1,2,0:T(8,128)S(1)}, f32[5,8,2,128]{3,1,2,0:T(8,128)S(1)}, u32[]{:S(2)}, u32[]{:S(2)}) collective-permute-start(f32[5,8,2,128]{3,1,2,0:T(8,128)S(1)} %copy.70), channel_id=1, source_target_pairs={{1,0},{2,1},{3,2},{4,3},{5,4},{6,5},{7,6},{8,7},{9,8},{10,9},{11,1... | collective-permute-start | bytes 122888 | tf_op jit(solution)/shard_map/ppermute | solution.py:27
  204.1 13.8 %collective-permute-start.3 = (f32[5,8,2,128]{3,1,2,0:T(8,128)}, f32[5,8,2,128]{3,1,2,0:T(8,128)}, u32[]{:S(2)}, u32[]{:S(2)}) collective-permute-start(f32[5,8,2,128]{3,1,2,0:T(8,128)} %copy.72), channel_id=1, source_target_pairs={{0,1},{1,2},{2,3},{3,4},{4,5},{5,6},{6,7},{7,8},{8,9},{9,10},{10,1... | collective-permute-start | bytes 122888 | tf_op jit(solution)/shard_map/ppermute | solution.py:26
  208.0 11.1 %collective-permute-start = (f32[5,2,64,128]{3,2,1,0:T(8,128)}, f32[5,2,64,128]{3,2,1,0:T(8,128)S(1)}, u32[]{:S(2)}, u32[]{:S(2)}) collective-permute-start(f32[5,2,64,128]{3,2,1,0:T(8,128)} %get-tuple-element.35), channel_id=1, source_target_pairs={{16,0},{32,16},{48,32},{64,48},{80,64},{96,80},{112,96},{128,112},... | collective-permute-start | bytes 983048 | tf_op jit(solution)/shard_map/ppermute | solution.py:27
  209.3 10.7 %collective-permute-start.1 = (f32[5,2,64,128]{3,2,1,0:T(8,128)}, f32[5,2,64,128]{3,2,1,0:T(8,128)}, u32[]{:S(2)}, u32[]{:S(2)}) collective-permute-start(f32[5,2,64,128]{3,2,1,0:T(8,128)} %get-tuple-element.36), channel_id=1, source_target_pairs={{0,16},{16,32},{32,48},{48,64},{64,80},{80,96},{96,112},{112,128},... | collective-permute-start | bytes 983048 | tf_op jit(solution)/shard_map/ppermute | solution.py:26
  216.3 3.6 copy-start.3
  216.4 3.6 copy-start.8
  216.4 3.6 copy-start.11
  224.1 6.9 %copy-start.9 = (f32[513]{0:T(1024)S(1)}, f32[513]{0:T(1024)}, u32[]{:S(2)}) copy-start(f32[513]{0:T(1024)} %iota_convert_fusion) | copy-start | bytes 6160
  224.1 6.9 %copy-start.10 = (f32[513]{0:T(1024)S(1)}, f32[513]{0:T(1024)}, u32[]{:S(2)}) copy-start(f32[513]{0:T(1024)} %select_multiply_fusion) | copy-start | bytes 6160
  224.1 6.9 %copy-start.12 = (s32[4]{0:T(128)S(1)}, s32[4]{0:T(128)}, u32[]{:S(2)}) copy-start(s32[4]{0:T(128)} %and_select_fusion) | copy-start | bytes 52
  224.1 6.9 %copy-start.13 = (f32[8]{0:T(128)S(1)}, f32[8]{0:T(128)}, u32[]{:S(2)}) copy-start(f32[8]{0:T(128)} %add_multiply_fusion) | copy-start | bytes 100
  225.5 12.8 %all-to-all-start = ((f32[16,1,1280]{2,1,0:T(1,128)}), f32[16,1,1280]{2,1,0:T(1,128)S(1)}, u32[]{:S(2)}, u32[]{:S(2)}) async-start(f32[16,1,1280]{2,1,0:T(1,128)} %reshape.112), calls=%async_computation | async-start | bytes 163840 | tf_op jit(solution)/shard_map/all_to_all | solution.py:138
  285.7 375.7 %all-to-all-start.1 = ((f32[16,1,1280]{2,1,0:T(1,128)}), f32[16,1,1280]{2,1,0:T(1,128)S(1)}, u32[]{:S(2)}, u32[]{:S(2)}) async-start(f32[16,1,1280]{2,1,0:T(1,128)} %reshape.114), calls=%async_computation.1 | async-start | bytes 163840 | tf_op jit(solution)/shard_map/all_to_all | solution.py:142
Sparse Core Ops, SparseCore 0:
  189.5 469.9 all-reduce.3
where the time goes:
time: 677 us; the launch traced here: 676 us
  waiting for transfers between devices  378 us (56%)
  other arithmetic  191 us (28%)
  matrix products  39.7 us (6%)
  starting transfers between devices  26 us (4%)
  local copies, waits for them, and re-layouts  25.5 us (4%)
  between operations  15.1 us (2%)
    unnamed x2, waiting for transfers between devices  370 us
    scatter-add x1, other arithmetic, on_device(): jax.ops.segment_sum(contrib.reshape(-1), segment.reshape(-1), num_segment...  171 us
  transfers between devices with their start and end apart: 7, of which 4 were waited for; matrix products, arithmetic and copies ran while one was open for 10% of the time, Pallas kernels for 0%

commit v1 on v0

--- a/solution.py
+++ b/solution.py
@@ -2,14 +2,17 @@
 
 import jax
 import jax.numpy as jnp
+import numpy as np
 from jax import lax
+from jax.experimental import pallas as pl
+from jax.experimental.pallas import tpu as pltpu
 from jax.sharding import PartitionSpec as P
 
 AZIMUTH = 1024
 CYCLES = 8
 OBSERVERS = 64
 BINS = 1024
-
+MESH = pl.DeviceIdType.MESH
 
 gas_factor = 0.4
 time_step = 0.02
@@ -71,41 +74,195 @@
     return (8.0 * near_diff - far_diff) / 12.0
 
 
-def cycle_weights(length):
-    modes = jnp.arange(length // 2 + 1).astype(jnp.float32)
-    cutoff = 4.0 * (jnp.arange(CYCLES).astype(jnp.float32) + 1.0)
-    return jnp.exp(-((modes[None, :] / cutoff[:, None]) ** 8))
-
-
-def apply_filter(line_block, cycle_index, length):
-    half = length // 2 + 1
-    sample = jnp.arange(length)
-    modes = jnp.arange(half)
-    phase = (sample[:, None] * modes[None, :] % length).astype(jnp.float32) * (
-        2.0 * math.pi / length
-    )
-    cos_table = jnp.cos(phase)
-    sin_table = jnp.sin(phase)
-    factor = jnp.where((modes == 0) | (modes == length // 2), 1.0, 2.0) / length
-    selector = (cycle_index[:, None] == jnp.arange(CYCLES)[None, :]).astype(jnp.float32)
-    line_weight = (
-        jnp.dot(selector, cycle_weights(length), precision=lax.Precision.HIGHEST) * factor[None, :]
-    )
-    real_part = jnp.einsum("fln,nm->flm", line_block, cos_table, precision=lax.Precision.HIGHEST)
-    imag_part = jnp.einsum("fln,nm->flm", line_block, sin_table, precision=lax.Precision.HIGHEST)
-    smooth = jnp.einsum(
-        "flm,nm->fln", real_part * line_weight[None], cos_table, precision=lax.Precision.HIGHEST
-    )
-    smooth = smooth + jnp.einsum(
-        "flm,nm->fln", imag_part * line_weight[None], sin_table, precision=lax.Precision.HIGHEST
-    )
-    return smooth
+def filter_rows():
+    n = AZIMUTH
+    modes = np.arange(n // 2 + 1, dtype=np.float64)
+    lag = np.arange(n)
+    factor = np.where((modes == 0) | (modes == n // 2), 1.0, 2.0) / n
+    table = np.cos((modes[:, None] * lag[None, :]) % n * (2.0 * np.pi / n))
+    rows = np.zeros((CYCLES, 8, n), np.float32)
+    for j in range(CYCLES):
+        weight = np.exp(-((modes / (4.0 * (j + 1))) ** 8)) * factor
+        h = weight @ table
+        for r in range(8):
+            rows[j, r] = np.roll(h, r)
+    return rows
+
+
+def pieces_of(value, count):
+    out = []
+    for _ in range(count - 1):
+        part = value.astype(jnp.bfloat16)
+        out.append(part)
+        value = value - part.astype(jnp.float32)
+    out.append(value.astype(jnp.bfloat16))
+    return out
+
+
+def dot_t(a, b):
+    return lax.dot_general(a, b, (((1,), (1,)), ((), ())), preferred_element_type=jnp.float32)
+
+
+def sums_kernel(count_ref, q_ref, cells_ref, bins_ref, amp_ref, out_ref):
+    rows, lanes = q_ref.shape[1:]
+    slots = cells_ref.shape[1]
+    rho = q_ref[0]
+    m1, m2, m3 = q_ref[1], q_ref[2], q_ref[3]
+    kinetic = 0.5 * (m1 * (m1 / rho) + m2 * (m2 / rho) + m3 * (m3 / rho))
+    excess = gas_factor * (q_ref[4] - kinetic) - ref_pressure
+    parts = jnp.concatenate(pieces_of(excess.T, 3), axis=0)
+    cells = cells_ref[...]
+    row_hot = lax.broadcasted_iota(jnp.int32, (rows, slots), 0) == (cells >> 7)
+    row_hot = jnp.where(row_hot, 1.0, 0.0).astype(jnp.bfloat16)
+    picked = jnp.dot(parts, row_hot, preferred_element_type=jnp.float32)
+    picked = picked[:lanes] + picked[lanes : 2 * lanes] + picked[2 * lanes :]
+    lane_hot = lax.broadcasted_iota(jnp.int32, (lanes, slots), 0) == (cells & 127)
+    sampled = jnp.sum(jnp.where(lane_hot, picked, 0.0), axis=0, keepdims=True)
+    live = lax.broadcasted_iota(jnp.int32, (1, slots), 1) < count_ref[0]
+    sampled = jnp.where(live, sampled, 0.0)
+    owner_rows = lax.broadcasted_iota(jnp.int32, (16, slots), 0)
+    rest_rows = lax.broadcasted_iota(jnp.int32, (64, slots), 0)
+
+    def pair(i, carry):
+        halves = []
+        for top in range(2):
+            o = top * 32 + i
+            b = bins_ref[pl.ds(o, 1), :]
+            contrib = sampled * amp_ref[pl.ds(o, 1), :]
+            hit = owner_rows == ((b >> 1) & 15)
+            left = jnp.concatenate(
+                [
+                    jnp.where(hit, part.astype(jnp.float32), 0.0).astype(jnp.bfloat16)
+                    for part in pieces_of(contrib, 2)
+                ],
+                axis=0,
+            )
+            right = jnp.where(rest_rows == (((b & 1) << 5) | (b >> 5)), 1.0, 0.0).astype(
+                jnp.bfloat16
+            )
+            both = dot_t(left, right)
+            halves.append(both[:16] + both[16:])
+        out_ref[:, pl.ds(i, 1), :] = jnp.concatenate(halves, axis=1).reshape(16, 1, 128)
+        return carry
+
+    lax.fori_loop(0, 32, pair, 0, unroll=4)
+
+
+def reduce_kernel(p_ref, out_ref, got1, got2, rows2, send1, recv1, send2, recv2):
+    ax, az = lax.axis_index("ax"), lax.axis_index("az")
+    n_ax, n_az = 32, 16
+    barrier = pltpu.get_barrier_semaphore()
+    for r in range(1, n_az):
+        pl.semaphore_signal(
+            barrier, inc=1, device_id=(ax, lax.rem(az + r, n_az)), device_id_type=MESH
+        )
+    for r in range(1, n_ax):
+        pl.semaphore_signal(
+            barrier, inc=1, device_id=(lax.rem(ax + r, n_ax), az), device_id_type=MESH
+        )
+    pl.semaphore_wait(barrier, n_az - 1 + n_ax - 1)
+    first = []
+    for r in range(1, n_az):
+        peer = lax.rem(az + r, n_az)
+        copy = pltpu.make_async_remote_copy(
+            src_ref=p_ref.at[peer],
+            dst_ref=got1.at[r - 1],
+            send_sem=send1.at[r - 1],
+            recv_sem=recv1.at[r - 1],
+            device_id=(ax, peer),
+            device_id_type=MESH,
+        )
+        copy.start()
+        first.append(copy)
+    total = p_ref[az]
+    for r in range(1, n_az):
+        first[r - 1].wait_recv()
+        total = total + got1[r - 1]
+    turned = total.T
+    rows2[...] = jnp.concatenate(
+        [turned[(top * 2 + e) * 32 : (top * 2 + e) * 32 + 32] for e in range(2) for top in range(2)],
+        axis=1,
+    ).reshape(n_ax, 1, 128)
+    second = []
+    for r in range(1, n_ax):
+        peer = lax.rem(ax + r, n_ax)
+        copy = pltpu.make_async_remote_copy(
+            src_ref=rows2.at[peer],
+            dst_ref=got2.at[r - 1],
+            send_sem=send2.at[r - 1],
+            recv_sem=recv2.at[r - 1],
+            device_id=(peer, az),
+            device_id_type=MESH,
+        )
+        copy.start()
+        second.append(copy)
+    total = rows2[ax]
+    for r in range(1, n_ax):
+        second[r - 1].wait_recv()
+        total = total + got2[r - 1]
+    out_ref[...] = total
+    for copy in first + second:
+        copy.wait_send()
+
+
+def filter_kernel(x_ref, h_ref, out_ref):
+    h = h_ref[...]
+    g = jnp.concatenate([h if k == 0 else pltpu.roll(h, 8 * k, 1) for k in range(16)], axis=0)
+    g_hi, g_lo = pieces_of(g, 2)
+    x = x_ref[...]
+    lines = x.shape[0]
+    turned = jnp.concatenate(
+        [
+            x if a == 0 else jnp.concatenate([x[:, 128 * a :], x[:, : 128 * a]], axis=1)
+            for a in range(8)
+        ],
+        axis=0,
+    )
+    x_hi, x_lo = pieces_of(turned, 2)
+    y = dot_t(x_hi, g_hi) + (dot_t(x_lo, g_hi) + dot_t(x_hi, g_lo))
+    for a in range(8):
+        out_ref[:, 128 * a : 128 * a + 128] = y[a * lines : (a + 1) * lines]
 
 
 def on_device(conserved, panel_cells, panel_counts, time_bins, amplitudes):
     planes_dev = conserved.shape[1]
     sector = conserved.shape[2]
     radial_all = conserved.shape[3]
+    slots = panel_cells.shape[0]
+    vmem = pl.BlockSpec(memory_space=pltpu.VMEM)
+    smem = pl.BlockSpec(memory_space=pltpu.SMEM)
+    partial_signal = pl.pallas_call(
+        sums_kernel,
+        out_shape=jax.ShapeDtypeStruct((16, 32, 128), jnp.float32),
+        in_specs=[smem] + [vmem] * 4,
+        out_specs=vmem,
+        name="sums",
+    )(
+        panel_counts,
+        conserved.reshape(5, planes_dev * sector, radial_all),
+        panel_cells.reshape(1, slots),
+        time_bins.T,
+        amplitudes.T,
+    )
+    signal = pl.pallas_call(
+        reduce_kernel,
+        out_shape=jax.ShapeDtypeStruct((1, 128), jnp.float32),
+        in_specs=[vmem],
+        out_specs=vmem,
+        scratch_shapes=[
+            pltpu.VMEM((15, 32, 128), jnp.float32),
+            pltpu.VMEM((31, 1, 128), jnp.float32),
+            pltpu.VMEM((32, 1, 128), jnp.float32),
+            pltpu.SemaphoreType.DMA((15,)),
+            pltpu.SemaphoreType.DMA((15,)),
+            pltpu.SemaphoreType.DMA((31,)),
+            pltpu.SemaphoreType.DMA((31,)),
+        ],
+        compiler_params=pltpu.CompilerParams(collective_id=0, has_side_effects=True),
+        name="reduce",
+    )(partial_signal)
+    signal = signal.reshape(2, OBSERVERS).T
+
     primitive = primitives(conserved)
     radius = jnp.arange(radial_all).astype(jnp.float32) + 0.5
     dtheta = 2.0 * math.pi / AZIMUTH
@@ -133,26 +290,27 @@
         ]
     )
     raw_section = conserved + time_step * (tendency + source)
-    inner = raw_section[..., :CYCLES]
-    lines = jnp.transpose(inner, (0, 1, 3, 2)).reshape(5, planes_dev * CYCLES, sector)
-    line_block = lax.all_to_all(lines, "az", split_axis=1, concat_axis=2, tiled=True)
-    line_count = line_block.shape[1]
-    cycle_index = (lax.axis_index("az") * line_count + jnp.arange(line_count)) % CYCLES
-    smooth = apply_filter(line_block, cycle_index, AZIMUTH)
-    filtered = lax.all_to_all(smooth, "az", split_axis=2, concat_axis=1, tiled=True)
-    filtered = jnp.transpose(filtered.reshape(5, planes_dev, CYCLES, sector), (0, 1, 3, 2))
+    inner = raw_section[..., :CYCLES].reshape(5, 2, planes_dev // 2, sector, CYCLES)
+    lines = jnp.transpose(inner, (4, 1, 0, 2, 3)).reshape(16, 20, sector)
+    lines = lax.all_to_all(lines, "az", split_axis=0, concat_axis=0, tiled=True)
+    lines = jnp.transpose(lines, (1, 0, 2)).reshape(20, AZIMUTH)
+    lines = jnp.pad(lines, ((0, 4), (0, 0)))
+    rows = lax.dynamic_index_in_dim(
+        jnp.asarray(filter_rows()), lax.axis_index("az") // 2, 0, keepdims=False
+    )
+    smooth = pl.pallas_call(
+        filter_kernel,
+        out_shape=jax.ShapeDtypeStruct((24, AZIMUTH), jnp.float32),
+        in_specs=[vmem] * 2,
+        out_specs=vmem,
+        name="filter",
+    )(lines, rows)
+    smooth = jnp.transpose(smooth[:20].reshape(20, 16, sector), (1, 0, 2))
+    smooth = lax.all_to_all(smooth, "az", split_axis=0, concat_axis=0, tiled=True)
+    filtered = jnp.transpose(
+        smooth.reshape(CYCLES, 2, 5, planes_dev // 2, sector), (2, 1, 3, 4, 0)
+    ).reshape(5, planes_dev, sector, CYCLES)
     section = jnp.concatenate([filtered, raw_section[..., CYCLES:]], axis=3)
-    slot_count = panel_cells.shape[0]
-    live = jnp.arange(slot_count) < panel_counts[0]
-    sampled = jnp.where(live, thermo_stress_level.reshape(-1)[panel_cells] - ref_pressure, 0.0)
-    contrib = sampled[:, None] * amplitudes
-    segment = jnp.arange(OBSERVERS)[None, :] * BINS + time_bins
-    partial_signal = jax.ops.segment_sum(
-        contrib.reshape(-1), segment.reshape(-1), num_segments=OBSERVERS * BINS
-    )
-    signal = lax.psum_scatter(
-        partial_signal.reshape(OBSERVERS, BINS), ("ax", "az"), scatter_dimension=1, tiled=True
-    )
     return (section, signal)
 
 

time: 677 us -> 106 us (0.16)
  waiting for transfers between devices: 378 us -> 9.01 us
  other arithmetic: 191 us -> 16.9 us
  Pallas kernels: 0 us -> 42.7 us
  matrix products: 39.7 us -> 0 us
  local copies, waits for them, and re-layouts: 25.5 us -> 10.3 us
  between operations: 15.1 us -> 1.51 us
    unnamed x2 -> x0, waiting for transfers between devices: 370 us -> none
    scatter-add x1 -> x0, other arithmetic: 171 us -> none  [on_device(): jax.ops.segment_sum(contrib.reshape(-1), segment.reshape(-1), num_segment...]
    pallas_call x0 -> x3, Pallas kernels: none -> 42.7 us  [the longest x1 35.3 us: on_device(): pl.pallas_call(reduce_kernel, out_shape=jax.ShapeDtypeStruct((1, 128), jn...]
    dot_general x5 -> x0, matrix products: 39.7 us -> none  [the longest x1 10.2 us: apply_filter(): jnp.einsum('fln,nm->flm', line_block, sin_table, precision=lax.Precision....]
    unnamed x34 -> x12, local copies, waits for them, and re-layouts: 11.1 us -> 1.92 us
  transfers between devices with their start and end apart: 7 -> 6, of which waited for: 4 -> 3; matrix products, arithmetic and copies ran while one was open for 10% -> 8% of each run, Pallas kernels for 0% -> 38%
where the time goes in v1:
time: 106 us
  Pallas kernels  42.7 us (40%)
  starting transfers between devices  25.4 us (24%)
  other arithmetic  16.9 us (16%)
  local copies, waits for them, and re-layouts  10.3 us (10%)
  waiting for transfers between devices  9.01 us (8%)
  between operations  1.51 us (1%)
    pallas_call x1, Pallas kernels, on_device(): pl.pallas_call(reduce_kernel, out_shape=jax.ShapeDtypeStruct((1, 128), jn...  35.3 us
    ppermute x2, starting transfers between devices, padded_2(): after = lax.ppermute(leading, axis, down)  10 us
    add x1, other arithmetic, on_device(): raw_section = conserved + time_step * (tendency + source)  7.44 us
    ppermute x2, starting transfers between devices, padded_2(): before = lax.ppermute(last, axis, up)  6.65 us
    all_to_all x1, waiting for transfers between devices, on_device(): lines = lax.all_to_all(lines, 'az', split_axis=0, concat_axis=0, tiled=True)  6.03 us
    pallas_call x1, Pallas kernels, on_device(): pl.pallas_call(sums_kernel, out_shape=jax.ShapeDtypeStruct((16, 32, 128),...  5.26 us
    all_to_all x1, starting transfers between devices, on_device(): lines = lax.all_to_all(lines, 'az', split_axis=0, concat_axis=0, tiled=True)  4.93 us
    all_to_all x1, starting transfers between devices, on_device(): lax.all_to_all(smooth, 'az', split_axis=0, concat_axis=0, tiled=True)  3.8 us
  transfers between devices with their start and end apart: 6, of which 3 were waited for; matrix products, arithmetic and copies ran while one was open for 8% of the time, Pallas kernels for 38%

profile of v1, /device:TPU:1, one launch (start us, length us, event | category | flops | bytes accessed | tf_op | source)
XLA Modules:
  0.0 105.7 jit_solution(8543244097896906270)
XLA Ops:
  0.6 0.0 copy-start.3
  0.6 1.1 %constant_dynamic-update-slice_fusion = (f32[5,8,64,128]{3,2,1,0:T(8,128)S(1)}, f32[1,8,64,128]{3,2,1,0:T(8,128)S(1)}) fusion(f32[5,8,64,128]{3,2,1,0:T(8,128)} %param.6), kind=kLoop, calls=%fused_computation.67 | loop fusion | flops 131071 | bytes 1048576
  1.7 0.0 copy-start
  1.8 1.5 %add_dynamic-update-slice_fusion.1 = (f32[5,8,64,128]{3,2,1,0:T(8,128)S(1)}, f32[1,8,64,128]{3,2,1,0:T(8,128)S(1)}, f32[1,8,64,128]{3,2,1,0:T(8,128)S(1)}, f32[1,8,64,128]{3,2,1,0:T(8,128)S(1)}) fusion(f32[5,8,64,128]{3,2,1,0:T(8,128)S(1)} %get-tuple-element.8, f32[1,8,64,128]{3,2,1,0:T(8,128)S(1)} %get-tuple-element.9, f32[5,8,64,128]{3,2,1,0:T(8,128)} %param.6), kind=kLoop, calls=%fused_computation.57 | loop fusion | flops 851968 | bytes 2621440
  3.3 0.2 copy-done
  3.5 0.1 multiply_dynamic-update-slice_fusion.5
  3.6 0.1 multiply_dynamic-update-slice_fusion.7
  3.7 0.3 multiply_dynamic-update-slice_fusion.4
  4.0 0.0 copy-start.1
  4.0 0.1 constant_dynamic-update-slice_fusion.2
  4.1 0.1 multiply_dynamic-update-slice_fusion.3
  4.1 0.0 copy-start.2
  4.2 8.7 %collective-permute-start.2 = (f32[5,8,2,128]{3,2,1,0:T(2,128)S(1)}, f32[5,8,2,128]{3,2,1,0:T(2,128)}, u32[]{:S(2)}, u32[]{:S(2)}) collective-permute-start(f32[5,8,2,128]{3,2,1,0:T(2,128)S(1)} %get-tuple-element.24), channel_id=1, source_target_pairs={{1,0},{2,1},{3,2},{4,3},{5,4},{6,5},{7,6},{8,7},{9,8},{10,9},{11,1... | collective-permute-start | bytes 122888 | tf_op jit(solution)/shard_map/ppermute | solution.py:30
  12.9 1.9 %collective-permute-start.3 = (f32[5,8,2,128]{3,2,1,0:T(2,128)S(1)}, f32[5,8,2,128]{3,2,1,0:T(2,128)}, u32[]{:S(2)}, u32[]{:S(2)}) collective-permute-start(f32[5,8,2,128]{3,2,1,0:T(2,128)S(1)} %get-tuple-element.25), channel_id=1, source_target_pairs={{0,1},{1,2},{2,3},{3,4},{4,5},{5,6},{6,7},{7,8},{8,9},{9,10},{10,1... | collective-permute-start | bytes 122888 | tf_op jit(solution)/shard_map/ppermute | solution.py:29
  14.9 0.9 fusion.25
  15.7 0.0 copy-done.1
  15.7 1.3 %collective-permute-start = (f32[5,2,64,128]{3,2,1,0:T(8,128)}, f32[5,2,64,128]{3,2,1,0:T(8,128)S(1)}, u32[]{:S(2)}, u32[]{:S(2)}) collective-permute-start(f32[5,2,64,128]{3,2,1,0:T(8,128)} %get-tuple-element.20), channel_id=1, source_target_pairs={{16,0},{32,16},{48,32},{64,48},{80,64},{96,80},{112,96},{128,112},... | collective-permute-start | bytes 983048 | tf_op jit(solution)/shard_map/ppermute | solution.py:30
  17.0 4.7 %collective-permute-start.1 = (f32[5,2,64,128]{3,2,1,0:T(8,128)}, f32[5,2,64,128]{3,2,1,0:T(8,128)}, u32[]{:S(2)}, u32[]{:S(2)}) collective-permute-start(f32[5,2,64,128]{3,2,1,0:T(8,128)} %get-tuple-element.21), channel_id=1, source_target_pairs={{0,16},{16,32},{32,48},{48,64},{64,80},{80,96},{96,112},{112,128},... | collective-permute-start | bytes 983048 | tf_op jit(solution)/shard_map/ppermute | solution.py:29
  21.8 0.0 copy-done.3
  21.8 1.2 %broadcast_multiply_fusion = f32[5,8,64,128]{3,2,1,0:T(8,128)} fusion(f32[5,8,64,128]{3,2,1,0:T(8,128)S(1)} %get-tuple-element.26, f32[128]{0:T(128)S(1)} %convert_add_fusion), kind=kLoop, calls=%fused_computation.43 | loop fusion | flops 327680 | bytes 2621952 | tf_op jit(solution)/shard_map/mul | solution.py:274
  22.9 0.0 copy-done.2
  22.9 0.5 broadcast_multiply_fusion.1
  23.5 0.6 pad.12.clone
  24.0 0.6 pad.15.clone
  24.6 0.0 collective-permute-done.2
  24.6 0.0 collective-permute-done.3
  24.6 2.0 %collective-permute-done = f32[5,2,64,128]{3,2,1,0:T(8,128)S(1)} collective-permute-done((f32[5,2,64,128]{3,2,1,0:T(8,128)}, f32[5,2,64,128]{3,2,1,0:T(8,128)S(1)}, u32[]{:S(2)}, u32[]{:S(2)}) %collective-permute-start) | collective-permute-done | bytes 327712 | tf_op jit(solution)/shard_map/ppermute | solution.py:30
  26.6 1.0 collective-permute-done.1
  27.6 7.4 %multiply_add_fusion = f32[5,8,64,128]{3,2,1,0:T(8,128)S(1)} fusion(f32[5,8,64,128]{3,2,1,0:T(8,128)S(1)} %copy-done, f32[1,8,64,128]{3,2,1,0:T(8,128)S(1)} %get-tuple-element.12, f32[1,8,64,128]{3,2,1,0:T(8,128)S(1)} %get-tuple-element.15, f32[5,8,64,128]{3,2,1,0:T(8,128)} %copy-done.2, f32[5,8,2,128]{3,2,1,0:T(2,128)} %collective-permute-done.3, ...), kind=kLoop, calls=%fused_computation.42 | loop fusion | flops 11141120 | bytes 7816232 | tf_op jit(solution)/shard_map/add | solution.py:292
  35.1 0.4 copy.19
  35.4 0.1 copy.20
  35.5 0.8 reshape.63
  36.3 4.9 %all-to-all-start = ((f32[16,1,1280]{2,1,0:T(1,128)}), f32[16,1,1280]{2,1,0:T(1,128)S(1)}, u32[]{:S(2)}, u32[]{:S(2)}) async-start(f32[16,1,1280]{2,1,0:T(1,128)} %reshape.63), calls=%async_computation | async-start | bytes 163840 | tf_op jit(solution)/shard_map/all_to_all | solution.py:295
  41.2 1.4 %dynamic-slice_bitcast_fusion.h_ref = f32[8,1024]{1,0:T(8,128)} fusion(f32[8,8,1024]{2,1,0:T(8,128)} %constant.50.clone, s32[]{:T(128)S(6)} %select_n.10), kind=kLoop, calls=%fused_computation.71 | loop fusion | bytes 65540 | tf_op jit(solution)/shard_map/jit(dynamic_index_in_dim)/squeeze | solution.py:298
  42.6 6.0 %all-to-all-done = f32[16,1,1280]{2,1,0:T(1,128)S(1)} async-done(((f32[16,1,1280]{2,1,0:T(1,128)}), f32[16,1,1280]{2,1,0:T(1,128)S(1)}, u32[]{:S(2)}, u32[]{:S(2)}) %all-to-all-start) | async-done | bytes 81952 | tf_op jit(solution)/shard_map/all_to_all | solution.py:295
  48.6 0.6 broadcast.88
  49.2 0.9 reduce.5
  50.1 0.1 reshape.64
  50.2 0.1 reshape.46
  50.3 0.7 pad.9.x_ref
  51.0 2.1 %filter.1 = f32[24,1024]{1,0:T(8,128)} custom-call(f32[24,1024]{1,0:T(8,128)} %pad.9.x_ref, f32[8,1024]{1,0:T(8,128)} %dynamic-slice_bitcast_fusion.h_ref), custom_call_target="tpu_custom_call" | custom-call | tf_op jit(solution)/shard_map/filter/pallas_call | solution.py:301
  53.1 1.0 reshape.47
  54.1 0.1 copy.28
  54.2 0.8 reshape.65
  54.9 3.8 %all-to-all-start.1 = ((f32[16,1,1280]{2,1,0:T(1,128)}), f32[16,1,1280]{2,1,0:T(1,128)S(1)}, u32[]{:S(2)}, u32[]{:S(2)}) async-start(f32[16,1,1280]{2,1,0:T(1,128)} %reshape.65), calls=%async_computation.1 | async-start | bytes 163840 | tf_op jit(solution)/shard_map/all_to_all | solution.py:309
  59.4 5.3 %sums.1.p_ref = f32[16,32,128]{2,1,0:T(8,128)} custom-call(s32[1]{0:T(128)S(6)} %copy.41.count_ref, f32[5,512,128]{2,1,0:T(8,128)} %bitcast.23, s32[1,512]{1,0:T(1,128)} %bitcast.33, s32[64,512]{1,0:T(8,128)} %bitcast.31, f32[64,512]{1,0:T(8,128)} %bitcast.32), custom_call_target="tpu_custom_call" | custom-call | tf_op jit(solution)/shard_map/sums/pallas_call | solution.py:234
  64.7 35.3 %reduce.7 = f32[1,128]{1,0:T(1,128)} custom-call(f32[16,32,128]{2,1,0:T(8,128)} %sums.1.p_ref), custom_call_target="tpu_custom_call" | custom-call | tf_op jit(solution)/shard_map/reduce/pallas_call | solution.py:247
  99.9 0.5 broadcast.84
  100.4 1.3 %reduce.4 = f32[128]{0:T(128)S(1)} reduce(f32[1,128]{1,0:T(1,128)} %reduce.7, f32[]{:T(128)} %broadcast.84), dimensions={0}, to_apply=%pallas_call.11.reduce_sub_computation.3 | reduce | bytes 1028 | tf_op jit(solution)/shard_map/reduce/pallas_call | solution.py:247
  101.7 0.6 reshape.52
  102.4 0.4 slice.121
  102.8 0.0 all-to-all-done.1
  102.8 0.9 reduce.6
  103.7 0.1 reshape.66
  103.8 0.4 copy.26
  104.2 1.5 %pad_maximum_fusion.4 = f32[5,8,64,128]{3,2,1,0:T(8,128)} fusion(f32[5,8,64,120]{3,2,1,0:T(8,128)S(1)} %slice.121, f32[5,8,64,8]{3,2,1,0:T(8,128)S(1)} %bitcast.25), kind=kLoop, calls=%fused_computation.41 | loop fusion | flops 327680 | bytes 2621440 | tf_op jit(solution)/shard_map/concatenate | solution.py:313
  (6 shorter events, 0.1 us)
Async XLA Ops:
  0.6 21.1 %copy-start.3 = (f32[128]{0:T(128)}, f32[128]{0:T(128)S(1)}, u32[]{:S(2)}) copy-start(f32[128]{0:T(128)S(1)} %convert_add_fusion) | copy-start | bytes 1540
  1.7 1.7 %copy-start = (f32[5,8,64,128]{3,2,1,0:T(8,128)S(1)}, f32[5,8,64,128]{3,2,1,0:T(8,128)}, u32[]{:S(2)}) copy-start(f32[5,8,64,128]{3,2,1,0:T(8,128)} %param.6) | copy-start | bytes 3932164
  4.0 11.7 %copy-start.1 = (f32[5,8,64,128]{3,2,1,0:T(8,128)}, f32[5,8,64,128]{3,2,1,0:T(8,128)S(1)}, u32[]{:S(2)}) copy-start(f32[5,8,64,128]{3,2,1,0:T(8,128)S(1)} %get-tuple-element.13) | copy-start | bytes 3932164
  4.1 18.8 %copy-start.2 = (f32[5,8,64,128]{3,2,1,0:T(8,128)}, f32[5,8,64,128]{3,2,1,0:T(8,128)S(1)}, u32[]{:S(2)}) copy-start(f32[5,8,64,128]{3,2,1,0:T(8,128)S(1)} %get-tuple-element.27) | copy-start | bytes 3932164
  4.2 20.5 %collective-permute-start.2 = (f32[5,8,2,128]{3,2,1,0:T(2,128)S(1)}, f32[5,8,2,128]{3,2,1,0:T(2,128)}, u32[]{:S(2)}, u32[]{:S(2)}) collective-permute-start(f32[5,8,2,128]{3,2,1,0:T(2,128)S(1)} %get-tuple-element.24), channel_id=1, source_target_pairs={{1,0},{2,1},{3,2},{4,3},{5,4},{6,5},{7,6},{8,7},{9,8},{10,9},{11,1... | collective-permute-start | bytes 122888 | tf_op jit(solution)/shard_map/ppermute | solution.py:30
  12.9 11.7 %collective-permute-start.3 = (f32[5,8,2,128]{3,2,1,0:T(2,128)S(1)}, f32[5,8,2,128]{3,2,1,0:T(2,128)}, u32[]{:S(2)}, u32[]{:S(2)}) collective-permute-start(f32[5,8,2,128]{3,2,1,0:T(2,128)S(1)} %get-tuple-element.25), channel_id=1, source_target_pairs={{0,1},{1,2},{2,3},{3,4},{4,5},{5,6},{6,7},{7,8},{8,9},{9,10},{10,1... | collective-permute-start | bytes 122888 | tf_op jit(solution)/shard_map/ppermute | solution.py:29
  15.7 10.9 %collective-permute-start = (f32[5,2,64,128]{3,2,1,0:T(8,128)}, f32[5,2,64,128]{3,2,1,0:T(8,128)S(1)}, u32[]{:S(2)}, u32[]{:S(2)}) collective-permute-start(f32[5,2,64,128]{3,2,1,0:T(8,128)} %get-tuple-element.20), channel_id=1, source_target_pairs={{16,0},{32,16},{48,32},{64,48},{80,64},{96,80},{112,96},{128,112},... | collective-permute-start | bytes 983048 | tf_op jit(solution)/shard_map/ppermute | solution.py:30
  17.0 10.6 %collective-permute-start.1 = (f32[5,2,64,128]{3,2,1,0:T(8,128)}, f32[5,2,64,128]{3,2,1,0:T(8,128)}, u32[]{:S(2)}, u32[]{:S(2)}) collective-permute-start(f32[5,2,64,128]{3,2,1,0:T(8,128)} %get-tuple-element.21), channel_id=1, source_target_pairs={{0,16},{16,32},{32,48},{48,64},{64,80},{80,96},{96,112},{112,128},... | collective-permute-start | bytes 983048 | tf_op jit(solution)/shard_map/ppermute | solution.py:29
  36.3 12.3 %all-to-all-start = ((f32[16,1,1280]{2,1,0:T(1,128)}), f32[16,1,1280]{2,1,0:T(1,128)S(1)}, u32[]{:S(2)}, u32[]{:S(2)}) async-start(f32[16,1,1280]{2,1,0:T(1,128)} %reshape.63), calls=%async_computation | async-start | bytes 163840 | tf_op jit(solution)/shard_map/all_to_all | solution.py:295
  54.9 47.8 %all-to-all-start.1 = ((f32[16,1,1280]{2,1,0:T(1,128)}), f32[16,1,1280]{2,1,0:T(1,128)S(1)}, u32[]{:S(2)}, u32[]{:S(2)}) async-start(f32[16,1,1280]{2,1,0:T(1,128)} %reshape.65), calls=%async_computation.1 | async-start | bytes 163840 | tf_op jit(solution)/shard_map/all_to_all | solution.py:309

commit v2 on v0

v2 whole, which is shorter than its diff:
```python
import math

import jax
import jax.numpy as jnp
import numpy as np
from jax import lax
from jax.experimental import pallas as pl
from jax.experimental.pallas import tpu as pltpu
from jax.sharding import PartitionSpec as P

AZIMUTH = 1024
CYCLES = 8
OBSERVERS = 64
BINS = 1024
MESH = pl.DeviceIdType.MESH

gas_factor = 0.4
time_step = 0.02
ref_pressure = 0.95


def filter_rows():
    n = AZIMUTH
    modes = np.arange(n // 2 + 1, dtype=np.float64)
    lag = np.arange(n)
    factor = np.where((modes == 0) | (modes == n // 2), 1.0, 2.0) / n
    table = np.cos((modes[:, None] * lag[None, :]) % n * (2.0 * np.pi / n))
    rows = np.zeros((CYCLES, 8, n), np.float32)
    for j in range(CYCLES):
        weight = np.exp(-((modes / (4.0 * (j + 1))) ** 8)) * factor
        h = weight @ table
        for r in range(8):
            rows[j, r] = np.roll(h, r)
    return rows


def pieces_of(value, count):
    out = []
    for _ in range(count - 1):
        part = value.astype(jnp.bfloat16)
        out.append(part)
        value = value - part.astype(jnp.float32)
    out.append(value.astype(jnp.bfloat16))
    return out


def dot_t(a, b):
    return lax.dot_general(a, b, (((1,), (1,)), ((), ())), preferred_element_type=jnp.float32)


def axis_ring(n, me, r):
    return lax.rem(me + r, n)


def step_kernel(
    count_ref,
    cells_ref,
    q_hbm,
    bins_hbm,
    amp_hbm,
    h_hbm,
    out_ref,
    sig_ref,
    q,
    bins,
    amp,
    h,
    axial,
    swirl,
    excess,
    edge_out,
    edge_in,
    inner,
    lines_out,
    lines_in,
    smooth_out,
    smooth_in,
    sums,
    sums_in,
    rows,
    rows_in,
    g_hi,
    g_lo,
    load_sem,
    near_send,
    near_recv,
    sums_send,
    sums_recv,
    rows_send,
    rows_recv,
    lines_send,
    lines_recv,
    smooth_send,
    smooth_recv,
):
    n_ax, n_az = 32, 16
    ax, az = lax.axis_index("ax"), lax.axis_index("az")

    def remote(source, target, send, recv, ax_to, az_to):
        return pltpu.make_async_remote_copy(
            src_ref=source,
            dst_ref=target,
            send_sem=send,
            recv_sem=recv,
            device_id=(ax_to, az_to),
            device_id_type=MESH,
        )

    loads = [
        pltpu.make_async_copy(q_hbm, q, load_sem.at[0]),
        pltpu.make_async_copy(bins_hbm, bins, load_sem.at[1]),
        pltpu.make_async_copy(amp_hbm, amp, load_sem.at[2]),
        pltpu.make_async_copy(h_hbm.at[lax.rem(az, CYCLES)], h, load_sem.at[3]),
    ]
    for copy in loads:
        copy.start()
    barrier = pltpu.get_barrier_semaphore()
    for r in range(1, n_ax):
        pl.semaphore_signal(
            barrier, inc=1, device_id=(axis_ring(n_ax, ax, r), az), device_id_type=MESH
        )
    for r in range(1, n_az):
        pl.semaphore_signal(
            barrier, inc=1, device_id=(ax, axis_ring(n_az, az, r)), device_id_type=MESH
        )

    lane = lax.broadcasted_iota(jnp.int32, (1, 128), 1)
    radius = lane.astype(jnp.float32) + 0.5
    over_r = 1.0 / radius
    step = jnp.float32(time_step)
    dtheta = 2.0 * math.pi / AZIMUTH
    near = (8.0 / 12.0) * step * over_r
    far = (1.0 / 12.0) * step * over_r
    plus_1 = jnp.where(lane < 127, -near, 0.0)
    minus_1 = jnp.where(lane > 0, near, 0.0)
    plus_2 = jnp.where(lane < 126, far, 0.0)
    minus_2 = jnp.where(lane > 1, -far, 0.0)
    swirl_gain = (-1.0 / 12.0) * step / (radius * dtheta)
    axial_gain = -time_step / 12.0

    loads[0].wait()

    def local(i, carry):
        p = i // 4
        at = pl.multiple_of((i % 4) * 16, 16)
        part = pl.ds(at, 16)
        q0, q1, q2, q3, q4 = [q[f, p, part, :] for f in range(5)]
        over = 1.0 / q0
        u, v, w = q1 * over, q2 * over, q3 * over
        pressure = gas_factor * (q4 - 0.5 * (q1 * u + q2 * v + q3 * w))
        excess[pl.ds(pl.multiple_of(i * 16, 16), 16), :] = pressure - ref_pressure
        total = q4 + pressure
        for f, value in enumerate((q1, q1 * u + pressure, q2 * u, q3 * u, total * u)):
            axial[p + 2, f, part, :] = value
        into = pl.ds(at + 8, 16)
        q3w = q3 * w
        for f, value in enumerate((q3, q1 * w, q2 * w, q3w + pressure, total * w)):
            swirl[f, p, into, :] = value
        q3v = q3 * v
        force = step * over_r
        old = (q0, q1, q2 + force * (pressure + q3w), q3 - force * q3v, q4)
        for f, value in enumerate((q2, q1 * v, q2 * v + pressure, q3v, total * v)):
            value = value * radius
            out_ref[f, p, part, :] = (
                old[f]
                + plus_1 * pltpu.roll(value, 127, 1)
                + minus_1 * pltpu.roll(value, 1, 1)
                + plus_2 * pltpu.roll(value, 126, 1)
                + minus_2 * pltpu.roll(value, 2, 1)
            )
        return carry

    lax.fori_loop(0, 32, local, 0, unroll=2)

    for f in range(5):
        for r in range(2):
            edge_out[0, f, r] = swirl[f, :, 8 + r, :]
            edge_out[1, f, r] = swirl[f, :, 70 + r, :]

    def turn_axial(f, carry):
        for a in range(4):
            tile = jnp.concatenate([axial[2 * a + 2, f], axial[2 * a + 3, f]], axis=0)
            inner[a + 1, f] = tile.T[:8]
        return carry

    lax.fori_loop(0, 5, turn_axial, 0)

    @pl.when(ax == 0)
    def _():
        inner[0] = jnp.zeros_like(inner[0])
        axial[0:2] = jnp.zeros((2, 5, 64, 128), jnp.float32)

    @pl.when(ax == n_ax - 1)
    def _():
        inner[5] = jnp.zeros_like(inner[5])
        axial[10:12] = jnp.zeros((2, 5, 64, 128), jnp.float32)

    slots = cells_ref.shape[1]
    parts = jnp.concatenate(pieces_of(excess[...].T, 3), axis=0)
    cells = cells_ref[...]
    row_hot = lax.broadcasted_iota(jnp.int32, (512, slots), 0) == (cells >> 7)
    row_hot = jnp.where(row_hot, 1.0, 0.0).astype(jnp.bfloat16)
    picked = jnp.dot(parts, row_hot, preferred_element_type=jnp.float32)
    picked = picked[:128] + picked[128:256] + picked[256:]
    lane_hot = lax.broadcasted_iota(jnp.int32, (128, slots), 0) == (cells & 127)
    sampled = jnp.sum(jnp.where(lane_hot, picked, 0.0), axis=0, keepdims=True)
    live = lax.broadcasted_iota(jnp.int32, (1, slots), 1) < count_ref[0]
    sampled = jnp.where(live, sampled, 0.0)
    owner_rows = lax.broadcasted_iota(jnp.int32, (16, slots), 0)
    rest_rows = lax.broadcasted_iota(jnp.int32, (64, slots), 0)
    loads[1].wait()
    loads[2].wait()

    def pair(i, carry):
        halves = []
        for top in range(2):
            o = top * 32 + i
            b = bins[pl.ds(o, 1), :]
            contrib = sampled * amp[pl.ds(o, 1), :]
            hit = owner_rows == ((b >> 1) & 15)
            left = jnp.concatenate(
                [
                    jnp.where(hit, piece.astype(jnp.float32), 0.0).astype(jnp.bfloat16)
                    for piece in pieces_of(contrib, 2)
                ],
                axis=0,
            )
            right = jnp.where(rest_rows == (((b & 1) << 5) | (b >> 5)), 1.0, 0.0).astype(
                jnp.bfloat16
            )
            both = dot_t(left, right)
            halves.append(both[:16] + both[16:])
        sums[:, pl.ds(i, 1), :] = jnp.concatenate(halves, axis=1).reshape(16, 1, 128)
        return carry

    lax.fori_loop(0, 32, pair, 0, unroll=4)

    pl.semaphore_wait(barrier, n_ax - 1 + n_az - 1)
    below, above = axis_ring(n_ax, ax, n_ax - 1), axis_ring(n_ax, ax, 1)
    left_az, right_az = axis_ring(n_az, az, n_az - 1), axis_ring(n_az, az, 1)
    edge_low = remote(
        edge_out.at[0], edge_in.at[1], near_send.at[0], near_recv.at[0], ax, left_az
    )
    edge_high = remote(
        edge_out.at[1], edge_in.at[0], near_send.at[1], near_recv.at[1], ax, right_az
    )
    inner_down = remote(inner.at[1], inner.at[5], near_send.at[2], near_recv.at[2], below, az)
    inner_up = remote(inner.at[4], inner.at[0], near_send.at[3], near_recv.at[3], above, az)
    halo_down = remote(
        axial.at[pl.ds(2, 2)],
        axial.at[pl.ds(10, 2)],
        near_send.at[4],
        near_recv.at[4],
        below,
        az,
    )
    halo_up = remote(
        axial.at[pl.ds(8, 2)],
        axial.at[pl.ds(0, 2)],
        near_send.at[5],
        near_recv.at[5],
        above,
        az,
    )
    edge_low.start()
    edge_high.start()

    @pl.when(ax > 0)
    def _():
        inner_down.start()
        halo_down.start()

    @pl.when(ax < n_ax - 1)
    def _():
        inner_up.start()
        halo_up.start()

    sums_copies = []
    for r in range(1, n_az):
        peer = axis_ring(n_az, az, r)
        copy = remote(
            sums.at[peer], sums_in.at[r - 1], sums_send.at[r - 1], sums_recv.at[r - 1], ax, peer
        )
        copy.start()
        sums_copies.append(copy)

    loads[3].wait()
    first = h[...]
    for k in range(16):
        g = first if k == 0 else pltpu.roll(first, 8 * k, 1)
        hi = g.astype(jnp.bfloat16).astype(jnp.float32)
        g_hi[8 * k : 8 * k + 8] = hi
        g_lo[8 * k : 8 * k + 8] = g - hi

    edge_low.wait_recv()
    edge_high.wait_recv()
    for f in range(5):
        for r in range(2):
            swirl[f, :, 6 + r, :] = edge_in[0, f, r]
            swirl[f, :, 72 + r, :] = edge_in[1, f, r]

    def around(p, carry):
        for f in range(5):
            out_ref[f, p] = out_ref[f, p] + swirl_gain * (
                8.0 * (swirl[f, p, 9:73, :] - swirl[f, p, 7:71, :])
                - (swirl[f, p, 10:74, :] - swirl[f, p, 6:70, :])
            )
        return carry

    lax.fori_loop(0, 8, around, 0)

    @pl.when(ax < n_ax - 1)
    def _():
        inner_down.wait_recv()

    @pl.when(ax > 0)
    def _():
        inner_up.wait_recv()

    upper = lane >= 64
    for d in range(n_az):
        lines_out[d, 8:16, :] = jnp.zeros((8, 128), jnp.float32)

    def turn_lines(f, carry):
        for a in range(4):
            tile = jnp.concatenate([out_ref[f, 2 * a], out_ref[f, 2 * a + 1]], axis=0)
            before, now, after = inner[a, f], inner[a + 1, f], inner[a + 2, f]
            next_1 = pltpu.roll(jnp.where(upper, now, after), 64, 1)
            last_1 = pltpu.roll(jnp.where(upper, before, now), 64, 1)
            line = tile.T[:8] + axial_gain * (8.0 * (next_1 - last_1) - (after - before))
            lines_out[
                pl.ds((a // 2) * 8, 8), pl.ds(f * 2 + a % 2, 1), :
            ] = line.reshape(8, 1, 128)
        return carry

    lax.fori_loop(0, 5, turn_lines, 0)
    lines_copies = []
    for r in range(1, n_az):
        peer = axis_ring(n_az, az, r)
        copy = remote(
            lines_out.at[peer], lines_in.at[az], lines_send.at[r - 1], lines_recv.at[r - 1], ax, peer
        )
        copy.start()
        lines_copies.append(copy)
    lines_in[az] = lines_out[az]

    total = sums[az]
    for r in range(1, n_az):
        sums_copies[r - 1].wait_recv()
        total = total + sums_in[r - 1]
    turned = total.T
    rows[...] = jnp.concatenate(
        [turned[(top * 2 + e) * 32 : (top * 2 + e) * 32 + 32] for e in range(2) for top in range(2)],
        axis=1,
    ).reshape(n_ax, 1, 128)
    rows_copies = []
    for r in range(1, n_ax):
        peer = axis_ring(n_ax, ax, r)
        copy = remote(
            rows.at[peer], rows_in.at[r - 1], rows_send.at[r - 1], rows_recv.at[r - 1], peer, az
        )
        copy.start()
        rows_copies.append(copy)

    @pl.when(ax < n_ax - 1)
    def _():
        halo_down.wait_recv()

    @pl.when(ax > 0)
    def _():
        halo_up.wait_recv()

    def along(p, carry):
        for f in range(5):
            out_ref[f, p] = out_ref[f, p] + axial_gain * (
                8.0 * (axial[p + 3, f] - axial[p + 1, f]) - (axial[p + 4, f] - axial[p, f])
            )
        return carry

    lax.fori_loop(0, 8, along, 0)

    for copy in lines_copies:
        copy.wait_recv()
    low, high = [], []
    for s in range(0, n_az, 2):
        one, two = lines_in[s], lines_in[s + 1]
        low.append(jnp.where(upper, pltpu.roll(two, 64, 1), one))
        high.append(jnp.where(upper, two, pltpu.roll(one, 64, 1)))
    x = jnp.concatenate(
        [jnp.concatenate(low, axis=1), jnp.concatenate(high, axis=1)], axis=0
    )
    turns = jnp.concatenate(
        [
            x if a == 0 else jnp.concatenate([x[:, 128 * a :], x[:, : 128 * a]], axis=1)
            for a in range(8)
        ],
        axis=0,
    )
    x_hi, x_lo = pieces_of(turns, 2)
    k_hi, k_lo = g_hi[...].astype(jnp.bfloat16), g_lo[...].astype(jnp.bfloat16)
    y = dot_t(x_hi, k_hi) + (dot_t(x_lo, k_hi) + dot_t(x_hi, k_lo))
    for a in range(8):
        one, two = y[32 * a : 32 * a + 16], y[32 * a + 16 : 32 * a + 32]
        smooth_out[2 * a] = jnp.where(upper, pltpu.roll(two, 64, 1), one)
        smooth_out[2 * a + 1] = jnp.where(upper, two, pltpu.roll(one, 64, 1))
    smooth_copies = []
    for r in range(1, n_az):
        peer = axis_ring(n_az, az, r)
        copy = remote(
            smooth_out.at[peer],
            smooth_in.at[az],
            smooth_send.at[r - 1],
            smooth_recv.at[r - 1],
            ax,
            peer,
        )
        copy.start()
        smooth_copies.append(copy)
    smooth_in[az] = smooth_out[az]
    for copy in smooth_copies:
        copy.wait_recv()
    cycles = lane < 8

    def turn_back(f, carry):
        for a in range(4):
            line = smooth_in[
                pl.ds((a // 2) * 8, 8), pl.ds(f * 2 + a % 2, 1), :
            ].reshape(8, 128)
            tile = jnp.concatenate([line, jnp.zeros((120, 128), jnp.float32)], axis=0).T
            for b in range(2):
                out_ref[f, 2 * a + b] = jnp.where(
                    cycles, tile[64 * b : 64 * b + 64], out_ref[f, 2 * a + b]
                )
        return carry

    lax.fori_loop(0, 5, turn_back, 0)
    total = rows[ax]
    for r in range(1, n_ax):
        rows_copies[r - 1].wait_recv()
        total = total + rows_in[r - 1]
    sig_ref[...] = total

    for copy in [edge_low, edge_high] + sums_copies + lines_copies + rows_copies + smooth_copies:
        copy.wait_send()

    @pl.when(ax > 0)
    def _():
        inner_down.wait_send()
        halo_down.wait_send()

    @pl.when(ax < n_ax - 1)
    def _():
        inner_up.wait_send()
        halo_up.wait_send()


def on_device(conserved, panel_cells, panel_counts, time_bins, amplitudes):
    f32 = jnp.float32
    vmem = pl.BlockSpec(memory_space=pltpu.VMEM)
    smem = pl.BlockSpec(memory_space=pltpu.SMEM)
    hbm = pl.BlockSpec(memory_space=pl.ANY)
    dma = pltpu.SemaphoreType.DMA
    section, signal = pl.pallas_call(
        step_kernel,
        out_shape=(
            jax.ShapeDtypeStruct(conserved.shape, f32),
            jax.ShapeDtypeStruct((1, 128), f32),
        ),
        in_specs=[smem, vmem, hbm, hbm, hbm, hbm],
        out_specs=(vmem, vmem),
        scratch_shapes=[
            pltpu.VMEM((5, 8, 64, 128), f32),
            pltpu.VMEM((64, 512), jnp.int32),
            pltpu.VMEM((64, 512), f32),
            pltpu.VMEM((8, 1024), f32),
            pltpu.VMEM((12, 5, 64, 128), f32),
            pltpu.VMEM((5, 8, 80, 128), f32),
            pltpu.VMEM((512, 128), f32),
            pltpu.VMEM((2, 5, 2, 8, 128), f32),
            pltpu.VMEM((2, 5, 2, 8, 128), f32),
            pltpu.VMEM((6, 5, 8, 128), f32),
            pltpu.VMEM((16, 16, 128), f32),
            pltpu.VMEM((16, 16, 128), f32),
            pltpu.VMEM((16, 16, 128), f32),
            pltpu.VMEM((16, 16, 128), f32),
            pltpu.VMEM((16, 32, 128), f32),
            pltpu.VMEM((15, 32, 128), f32),
            pltpu.VMEM((32, 1, 128), f32),
            pltpu.VMEM((31, 1, 128), f32),
            pltpu.VMEM((128, 1024), f32),
            pltpu.VMEM((128, 1024), f32),
            dma((4,)),
            dma((6,)),
            dma((6,)),
            dma((15,)),
            dma((15,)),
            dma((31,)),
            dma((31,)),
            dma((15,)),
            dma((15,)),
            dma((15,)),
            dma((15,)),
        ],
        compiler_params=pltpu.CompilerParams(collective_id=0, has_side_effects=True),
        name="step",
    )(
        panel_counts,
        panel_cells.reshape(1, panel_cells.shape[0]),
        conserved,
        time_bins.T,
        amplitudes.T,
        jnp.asarray(filter_rows()),
    )
    return (section, signal.reshape(2, OBSERVERS).T)


def solution(mesh):
    placed = (
        P(None, "ax", "az", None),
        P(("ax", "az")),
        P(("ax", "az")),
        P(("ax", "az"), None),
        P(("ax", "az"), None),
    )
    return jax.shard_map(
        on_device,
        mesh=mesh,
        in_specs=placed,
        out_specs=(P(None, "ax", "az", None), P(None, ("ax", "az"))),
        check_vma=False,
    )
```

time: 677 us -> 49.8 us (0.07)
  waiting for transfers between devices: 378 us -> 0 us
  other arithmetic: 191 us -> 1.3 us
  Pallas kernels: 0 us -> 43.3 us
  matrix products: 39.7 us -> 0 us
  starting transfers between devices: 26 us -> 0 us
  local copies, waits for them, and re-layouts: 25.5 us -> 3.68 us
  between operations: 15.1 us -> 1.29 us
    unnamed x2 -> x0, waiting for transfers between devices: 370 us -> none
    scatter-add x1 -> x0, other arithmetic: 171 us -> none  [on_device(): jax.ops.segment_sum(contrib.reshape(-1), segment.reshape(-1), num_segment...]
    pallas_call x0 -> x1, Pallas kernels: none -> 43.3 us  [on_device(): pl.pallas_call(step_kernel, out_shape=(jax.ShapeDtypeStruct(conserved.sha...]
    dot_general x5 -> x0, matrix products: 39.7 us -> none  [the longest x1 10.2 us: apply_filter(): jnp.einsum('fln,nm->flm', line_block, sin_table, precision=lax.Precision....]
    ppermute x4 -> x0, starting transfers between devices: 16.7 us -> none  [the longest x2 10 us: padded_2(): after = lax.ppermute(leading, axis, down)]
    all_to_all x2 -> x0, starting transfers between devices: 9.26 us -> none  [the longest x1 5.48 us: on_device(): lax.all_to_all(lines, 'az', split_axis=1, concat_axis=2, tiled=True)]
    unnamed x34 -> x1, local copies, waits for them, and re-layouts: 11.1 us -> 2.52 us
    all_to_all x2 -> x0, waiting for transfers between devices: 7.09 us -> none  [the longest x1 7.09 us: on_device(): lax.all_to_all(lines, 'az', split_axis=1, concat_axis=2, tiled=True)]
  transfers between devices with their start and end apart: 7 -> 0, of which waited for: 4 -> 0; matrix products, arithmetic and copies ran while one was open for 10% -> 0% of each run, Pallas kernels for 0% -> 0%
where the time goes in v2:
time: 49.8 us; the launch traced here: 49.6 us
  Pallas kernels  43.3 us (87%)
  local copies, waits for them, and re-layouts  3.68 us (7%)
  other arithmetic  1.3 us (3%)
  between operations  1.29 us (3%)
    pallas_call x1, Pallas kernels, on_device(): pl.pallas_call(step_kernel, out_shape=(jax.ShapeDtypeStruct(conserved.sha...  43.3 us
    unnamed x1, local copies, waits for them, and re-layouts  2.52 us
    pallas_call x1, other arithmetic, on_device(): pl.pallas_call(step_kernel, out_shape=(jax.ShapeDtypeStruct(conserved.sha...  1.3 us

profile of v2, /device:TPU:1, one launch (start us, length us, event | category | flops | bytes accessed | tf_op | source)
XLA Modules:
  0.0 49.6 jit_solution(11980980712620384055)
XLA Ops:
  1.3 43.3 %step.1 = (f32[5,8,64,128]{3,2,1,0:T(8,128)}, f32[1,128]{1,0:T(1,128)}) custom-call(s32[1]{0:T(128)S(6)} %copy.9.count_ref, s32[1,512]{1,0:T(1,128)} %bitcast.6, f32[5,8,64,128]{3,2,1,0:T(8,128)} %q_hbm.1, s32[64,512]{1,0:T(8,128)} %bitcast.4, f32[64,512]{1,0:T(8,128)} %bitcast.5, f32[8,8,1024]{2,1,0:T(8,128)} %constant.2.clone.h_hbm), custom_call_target="tpu_custom_call" | custom-call | tf_op jit(solution)/shard_map/step/pallas_call | solution.py:463
  44.6 0.5 %broadcast.3 = f32[]{:T(128)} broadcast(f32[]{:T(128)} %constant.8), dimensions={} | broadcast | bytes 8 | tf_op jit(solution)/shard_map/step/pallas_call | solution.py:463
  45.1 1.3 %reduce.3 = f32[128]{0:T(128)S(1)} reduce(f32[1,128]{1,0:T(1,128)} %get-tuple-element.5, f32[]{:T(128)} %broadcast.3), dimensions={0}, to_apply=%get-tuple-element.5.reduce_sub_computation.3 | reduce | bytes 1028 | tf_op jit(solution)/shard_map/step/pallas_call | solution.py:463
  46.4 0.6 %reshape.11 = f32[2,64]{1,0:T(2,128)} reshape(f32[128]{0:T(128)S(1)} %reduce.3) | data formatting | bytes 1024 | tf_op jit(solution)/shard_map/reshape | solution.py:514
  47.1 2.5 %copy.10 = f32[5,8,64,128]{3,2,1,0:T(8,128)} copy(f32[5,8,64,128]{3,2,1,0:T(8,128)} %get-tuple-element.8) | data formatting | bytes 2621440

commit v3 on v2

--- a/solution.py
+++ b/solution.py
@@ -53,14 +53,16 @@
 
 
 def step_kernel(
-    count_ref,
-    cells_ref,
+    count,
+    cells_hbm,
     q_hbm,
     bins_hbm,
     amp_hbm,
     h_hbm,
     out_ref,
     sig_ref,
+    raw,
+    cells_ref,
     q,
     bins,
     amp,
@@ -82,16 +84,11 @@
     g_hi,
     g_lo,
     load_sem,
+    plane_sem,
     near_send,
     near_recv,
-    sums_send,
-    sums_recv,
-    rows_send,
-    rows_recv,
-    lines_send,
-    lines_recv,
-    smooth_send,
-    smooth_recv,
+    bulk_send,
+    bulk_recv,
 ):
     n_ax, n_az = 32, 16
     ax, az = lax.axis_index("ax"), lax.axis_index("az")
@@ -107,15 +104,22 @@
         )
 
     loads = [
-        pltpu.make_async_copy(q_hbm, q, load_sem.at[0]),
+        pltpu.make_async_copy(cells_hbm, cells_ref, load_sem.at[0]),
         pltpu.make_async_copy(bins_hbm, bins, load_sem.at[1]),
         pltpu.make_async_copy(amp_hbm, amp, load_sem.at[2]),
         pltpu.make_async_copy(h_hbm.at[lax.rem(az, CYCLES)], h, load_sem.at[3]),
     ]
+
+    def plane_load(p):
+        return pltpu.make_async_copy(q_hbm.at[:, p], q.at[:, p], plane_sem.at[p])
+
+    for p in range(8):
+        plane_load(p).start()
     for copy in loads:
         copy.start()
     barrier = pltpu.get_barrier_semaphore()
-    for r in range(1, n_ax):
+    for k in range(1, n_ax):
+        r = n_ax // 2 + (k // 2 if k % 2 == 0 else -(k // 2))
         pl.semaphore_signal(
             barrier, inc=1, device_id=(axis_ring(n_ax, ax, r), az), device_id_type=MESH
         )
@@ -138,53 +142,44 @@
     swirl_gain = (-1.0 / 12.0) * step / (radius * dtheta)
     axial_gain = -time_step / 12.0
 
-    loads[0].wait()
-
-    def local(i, carry):
-        p = i // 4
-        at = pl.multiple_of((i % 4) * 16, 16)
-        part = pl.ds(at, 16)
-        q0, q1, q2, q3, q4 = [q[f, p, part, :] for f in range(5)]
-        over = 1.0 / q0
-        u, v, w = q1 * over, q2 * over, q3 * over
-        pressure = gas_factor * (q4 - 0.5 * (q1 * u + q2 * v + q3 * w))
-        excess[pl.ds(pl.multiple_of(i * 16, 16), 16), :] = pressure - ref_pressure
-        total = q4 + pressure
-        for f, value in enumerate((q1, q1 * u + pressure, q2 * u, q3 * u, total * u)):
-            axial[p + 2, f, part, :] = value
-        into = pl.ds(at + 8, 16)
-        q3w = q3 * w
-        for f, value in enumerate((q3, q1 * w, q2 * w, q3w + pressure, total * w)):
-            swirl[f, p, into, :] = value
-        q3v = q3 * v
-        force = step * over_r
-        old = (q0, q1, q2 + force * (pressure + q3w), q3 - force * q3v, q4)
-        for f, value in enumerate((q2, q1 * v, q2 * v + pressure, q3v, total * v)):
-            value = value * radius
-            out_ref[f, p, part, :] = (
-                old[f]
-                + plus_1 * pltpu.roll(value, 127, 1)
-                + minus_1 * pltpu.roll(value, 1, 1)
-                + plus_2 * pltpu.roll(value, 126, 1)
-                + minus_2 * pltpu.roll(value, 2, 1)
-            )
-        return carry
-
-    lax.fori_loop(0, 32, local, 0, unroll=2)
+
+    def local(p, carry):
+        plane_load(p).wait()
+        for at in range(0, 64, 16):
+            part = pl.ds(at, 16)
+            q0, q1, q2, q3, q4 = [q[f, p, part, :] for f in range(5)]
+            over = 1.0 / q0
+            u, v, w = q1 * over, q2 * over, q3 * over
+            pressure = gas_factor * (q4 - 0.5 * (q1 * u + q2 * v + q3 * w))
+            excess[pl.ds(pl.multiple_of(p * 64 + at, 16), 16), :] = pressure - ref_pressure
+            total = q4 + pressure
+            for f, value in enumerate((q1, q1 * u + pressure, q2 * u, q3 * u, total * u)):
+                axial[p + 2, f, part, :] = value
+            into = pl.ds(at + 8, 16)
+            q3w = q3 * w
+            for f, value in enumerate((q3, q1 * w, q2 * w, q3w + pressure, total * w)):
+                swirl[f, p, into, :] = value
+            q3v = q3 * v
+            force = step * over_r
+            old = (q0, q1, q2 + force * (pressure + q3w), q3 - force * q3v, q4)
+            for f, value in enumerate((q2, q1 * v, q2 * v + pressure, q3v, total * v)):
+                value = value * radius
+                raw[f, p, part, :] = (
+                    old[f]
+                    + plus_1 * pltpu.roll(value, 127, 1)
+                    + minus_1 * pltpu.roll(value, 1, 1)
+                    + plus_2 * pltpu.roll(value, 126, 1)
+                    + minus_2 * pltpu.roll(value, 2, 1)
+                )
+        return carry
+
+    lax.fori_loop(0, 8, local, 0)
 
     for f in range(5):
         for r in range(2):
             edge_out[0, f, r] = swirl[f, :, 8 + r, :]
             edge_out[1, f, r] = swirl[f, :, 70 + r, :]
 
-    def turn_axial(f, carry):
-        for a in range(4):
-            tile = jnp.concatenate([axial[2 * a + 2, f], axial[2 * a + 3, f]], axis=0)
-            inner[a + 1, f] = tile.T[:8]
-        return carry
-
-    lax.fori_loop(0, 5, turn_axial, 0)
-
     @pl.when(ax == 0)
     def _():
         inner[0] = jnp.zeros_like(inner[0])
@@ -196,6 +191,7 @@
         axial[10:12] = jnp.zeros((2, 5, 64, 128), jnp.float32)
 
     slots = cells_ref.shape[1]
+    loads[0].wait()
     parts = jnp.concatenate(pieces_of(excess[...].T, 3), axis=0)
     cells = cells_ref[...]
     row_hot = lax.broadcasted_iota(jnp.int32, (512, slots), 0) == (cells >> 7)
@@ -204,36 +200,45 @@
     picked = picked[:128] + picked[128:256] + picked[256:]
     lane_hot = lax.broadcasted_iota(jnp.int32, (128, slots), 0) == (cells & 127)
     sampled = jnp.sum(jnp.where(lane_hot, picked, 0.0), axis=0, keepdims=True)
-    live = lax.broadcasted_iota(jnp.int32, (1, slots), 1) < count_ref[0]
+    live = lax.broadcasted_iota(jnp.int32, (1, slots), 1) < count[0]
     sampled = jnp.where(live, sampled, 0.0)
-    owner_rows = lax.broadcasted_iota(jnp.int32, (16, slots), 0)
-    rest_rows = lax.broadcasted_iota(jnp.int32, (64, slots), 0)
+    sixteen = lax.broadcasted_iota(jnp.int32, (16, slots), 0)
+    ladder = [(sixteen + 16 * k).astype(jnp.float32).astype(jnp.bfloat16) for k in range(4)]
+    one, none = jnp.bfloat16(1.0), jnp.bfloat16(0.0)
+
+    def spread(value, k):
+        return jnp.broadcast_to(value[k : k + 1], (16, slots)).astype(jnp.bfloat16)
+
     loads[1].wait()
     loads[2].wait()
 
-    def pair(i, carry):
-        halves = []
+    def group(i, carry):
+        ready = []
         for top in range(2):
-            o = top * 32 + i
-            b = bins[pl.ds(o, 1), :]
-            contrib = sampled * amp[pl.ds(o, 1), :]
-            hit = owner_rows == ((b >> 1) & 15)
-            left = jnp.concatenate(
-                [
-                    jnp.where(hit, piece.astype(jnp.float32), 0.0).astype(jnp.bfloat16)
-                    for piece in pieces_of(contrib, 2)
-                ],
-                axis=0,
-            )
-            right = jnp.where(rest_rows == (((b & 1) << 5) | (b >> 5)), 1.0, 0.0).astype(
-                jnp.bfloat16
-            )
-            both = dot_t(left, right)
-            halves.append(both[:16] + both[16:])
-        sums[:, pl.ds(i, 1), :] = jnp.concatenate(halves, axis=1).reshape(16, 1, 128)
-        return carry
-
-    lax.fori_loop(0, 32, pair, 0, unroll=4)
+            at = pl.ds(pl.multiple_of(top * 32 + i * 8, 8), 8)
+            b = bins[at, :]
+            contrib = sampled * amp[at, :]
+            main = contrib.astype(jnp.bfloat16).astype(jnp.float32)
+            owner = ((b >> 1) & 15).astype(jnp.float32)
+            rest = (((b & 1) << 5) | (b >> 5)).astype(jnp.float32)
+            ready.append((main, contrib - main, owner, rest))
+        for k in range(8):
+            halves = []
+            for main, left_over, owner, rest in ready:
+                hit = spread(owner, k) == ladder[0]
+                left = jnp.concatenate(
+                    [jnp.where(hit, spread(part, k), none) for part in (main, left_over)], axis=0
+                )
+                place = spread(rest, k)
+                right = jnp.concatenate(
+                    [jnp.where(place == rung, one, none) for rung in ladder], axis=0
+                )
+                both = dot_t(left, right)
+                halves.append(both[:16] + both[16:])
+            sums[:, pl.ds(i * 8 + k, 1), :] = jnp.concatenate(halves, axis=1).reshape(16, 1, 128)
+        return carry
+
+    lax.fori_loop(0, 2, group, 0)
 
     pl.semaphore_wait(barrier, n_ax - 1 + n_az - 1)
     below, above = axis_ring(n_ax, ax, n_ax - 1), axis_ring(n_ax, ax, 1)
@@ -264,25 +269,38 @@
     )
     edge_low.start()
     edge_high.start()
+    def turn_axial(f, carry):
+        for a in range(4):
+            tile = jnp.concatenate([axial[2 * a + 2, f], axial[2 * a + 3, f]], axis=0)
+            inner[a + 1, f] = tile.T[:8]
+        return carry
+
+    lax.fori_loop(0, 5, turn_axial, 0)
+
 
     @pl.when(ax > 0)
     def _():
         inner_down.start()
+
+    @pl.when(ax < n_ax - 1)
+    def _():
+        inner_up.start()
+
+    @pl.when(ax > 0)
+    def _():
         halo_down.start()
 
-    @pl.when(ax < n_ax - 1)
-    def _():
-        inner_up.start()
+    @pl.when(jnp.logical_and(ax < n_ax - 1, ax != n_ax // 2 - 1))
+    def _():
         halo_up.start()
 
-    sums_copies = []
+    lax.fori_loop(2, 4, group, 0)
     for r in range(1, n_az):
         peer = axis_ring(n_az, az, r)
-        copy = remote(
-            sums.at[peer], sums_in.at[r - 1], sums_send.at[r - 1], sums_recv.at[r - 1], ax, peer
-        )
-        copy.start()
-        sums_copies.append(copy)
+        remote(sums.at[peer], sums_in.at[r - 1], bulk_send.at[0], bulk_recv.at[0], ax, peer).start()
+    all_sums = remote(
+        sums.at[pl.ds(0, 15)], sums_in, bulk_send.at[0], bulk_recv.at[0], ax, right_az
+    )
 
     loads[3].wait()
     first = h[...]
@@ -301,7 +319,7 @@
 
     def around(p, carry):
         for f in range(5):
-            out_ref[f, p] = out_ref[f, p] + swirl_gain * (
+            raw[f, p] = raw[f, p] + swirl_gain * (
                 8.0 * (swirl[f, p, 9:73, :] - swirl[f, p, 7:71, :])
                 - (swirl[f, p, 10:74, :] - swirl[f, p, 6:70, :])
             )
@@ -320,10 +338,11 @@
     upper = lane >= 64
     for d in range(n_az):
         lines_out[d, 8:16, :] = jnp.zeros((8, 128), jnp.float32)
+    lines_out = lines_out
 
     def turn_lines(f, carry):
         for a in range(4):
-            tile = jnp.concatenate([out_ref[f, 2 * a], out_ref[f, 2 * a + 1]], axis=0)
+            tile = jnp.concatenate([raw[f, 2 * a], raw[f, 2 * a + 1]], axis=0)
             before, now, after = inner[a, f], inner[a + 1, f], inner[a + 2, f]
             next_1 = pltpu.roll(jnp.where(upper, now, after), 64, 1)
             last_1 = pltpu.roll(jnp.where(upper, before, now), 64, 1)
@@ -334,53 +353,39 @@
         return carry
 
     lax.fori_loop(0, 5, turn_lines, 0)
-    lines_copies = []
     for r in range(1, n_az):
         peer = axis_ring(n_az, az, r)
-        copy = remote(
-            lines_out.at[peer], lines_in.at[az], lines_send.at[r - 1], lines_recv.at[r - 1], ax, peer
-        )
-        copy.start()
-        lines_copies.append(copy)
+        remote(
+            lines_out.at[peer], lines_in.at[az], bulk_send.at[1], bulk_recv.at[1], ax, peer
+        ).start()
+    most = pl.ds(0, 15)
+    all_lines = remote(
+        lines_out.at[most], lines_in.at[most], bulk_send.at[1], bulk_recv.at[1], ax, right_az
+    )
+
     lines_in[az] = lines_out[az]
 
+    all_sums.wait_recv()
     total = sums[az]
     for r in range(1, n_az):
-        sums_copies[r - 1].wait_recv()
         total = total + sums_in[r - 1]
     turned = total.T
     rows[...] = jnp.concatenate(
         [turned[(top * 2 + e) * 32 : (top * 2 + e) * 32 + 32] for e in range(2) for top in range(2)],
         axis=1,
     ).reshape(n_ax, 1, 128)
-    rows_copies = []
     for r in range(1, n_ax):
         peer = axis_ring(n_ax, ax, r)
-        copy = remote(
-            rows.at[peer], rows_in.at[r - 1], rows_send.at[r - 1], rows_recv.at[r - 1], peer, az
-        )
-        copy.start()
-        rows_copies.append(copy)
-
-    @pl.when(ax < n_ax - 1)
-    def _():
-        halo_down.wait_recv()
-
-    @pl.when(ax > 0)
-    def _():
-        halo_up.wait_recv()
-
-    def along(p, carry):
-        for f in range(5):
-            out_ref[f, p] = out_ref[f, p] + axial_gain * (
-                8.0 * (axial[p + 3, f] - axial[p + 1, f]) - (axial[p + 4, f] - axial[p, f])
-            )
-        return carry
-
-    lax.fori_loop(0, 8, along, 0)
-
-    for copy in lines_copies:
-        copy.wait_recv()
+        remote(rows.at[peer], rows_in.at[r - 1], bulk_send.at[2], bulk_recv.at[2], peer, az).start()
+    all_rows = remote(
+        rows.at[pl.ds(0, 31)], rows_in, bulk_send.at[2], bulk_recv.at[2], above, az
+    )
+
+    @pl.when(ax == n_ax // 2 - 1)
+    def _():
+        halo_up.start()
+
+    all_lines.wait_recv()
     low, high = [], []
     for s in range(0, n_az, 2):
         one, two = lines_in[s], lines_in[s + 1]
@@ -403,22 +408,33 @@
         one, two = y[32 * a : 32 * a + 16], y[32 * a + 16 : 32 * a + 32]
         smooth_out[2 * a] = jnp.where(upper, pltpu.roll(two, 64, 1), one)
         smooth_out[2 * a + 1] = jnp.where(upper, two, pltpu.roll(one, 64, 1))
-    smooth_copies = []
     for r in range(1, n_az):
         peer = axis_ring(n_az, az, r)
-        copy = remote(
-            smooth_out.at[peer],
-            smooth_in.at[az],
-            smooth_send.at[r - 1],
-            smooth_recv.at[r - 1],
-            ax,
-            peer,
-        )
-        copy.start()
-        smooth_copies.append(copy)
+        remote(
+            smooth_out.at[peer], smooth_in.at[az], bulk_send.at[3], bulk_recv.at[3], ax, peer
+        ).start()
+    all_smooth = remote(
+        smooth_out.at[most], smooth_in.at[most], bulk_send.at[3], bulk_recv.at[3], ax, right_az
+    )
     smooth_in[az] = smooth_out[az]
-    for copy in smooth_copies:
-        copy.wait_recv()
+    @pl.when(ax < n_ax - 1)
+    def _():
+        halo_down.wait_recv()
+
+    @pl.when(ax > 0)
+    def _():
+        halo_up.wait_recv()
+
+    def along(p, carry):
+        for f in range(5):
+            raw[f, p] = raw[f, p] + axial_gain * (
+                8.0 * (axial[p + 3, f] - axial[p + 1, f]) - (axial[p + 4, f] - axial[p, f])
+            )
+        return carry
+
+    lax.fori_loop(0, 8, along, 0)
+
+    all_smooth.wait_recv()
     cycles = lane < 8
 
     def turn_back(f, carry):
@@ -428,19 +444,22 @@
             ].reshape(8, 128)
             tile = jnp.concatenate([line, jnp.zeros((120, 128), jnp.float32)], axis=0).T
             for b in range(2):
-                out_ref[f, 2 * a + b] = jnp.where(
-                    cycles, tile[64 * b : 64 * b + 64], out_ref[f, 2 * a + b]
+                raw[f, 2 * a + b] = jnp.where(
+                    cycles, tile[64 * b : 64 * b + 64], raw[f, 2 * a + b]
                 )
         return carry
 
     lax.fori_loop(0, 5, turn_back, 0)
+    section_copy = pltpu.make_async_copy(raw, out_ref, load_sem.at[0])
+    section_copy.start()
+    all_rows.wait_recv()
     total = rows[ax]
     for r in range(1, n_ax):
-        rows_copies[r - 1].wait_recv()
         total = total + rows_in[r - 1]
-    sig_ref[...] = total
-
-    for copy in [edge_low, edge_high] + sums_copies + lines_copies + rows_copies + smooth_copies:
+    sig_ref[...] = jnp.concatenate([total[:, :64], total[:, 64:]], axis=0)
+
+    section_copy.wait()
+    for copy in (edge_low, edge_high, all_sums, all_lines, all_rows, all_smooth):
         copy.wait_send()
 
     @pl.when(ax > 0)
@@ -460,15 +479,21 @@
     smem = pl.BlockSpec(memory_space=pltpu.SMEM)
     hbm = pl.BlockSpec(memory_space=pl.ANY)
     dma = pltpu.SemaphoreType.DMA
+
+    def in_hbm(value):
+        return pltpu.with_memory_space_constraint(value, pltpu.HBM)
+
     section, signal = pl.pallas_call(
         step_kernel,
         out_shape=(
-            jax.ShapeDtypeStruct(conserved.shape, f32),
-            jax.ShapeDtypeStruct((1, 128), f32),
+            pltpu.VMEM(conserved.shape, f32),
+            jax.ShapeDtypeStruct((2, 64), f32),
         ),
-        in_specs=[smem, vmem, hbm, hbm, hbm, hbm],
-        out_specs=(vmem, vmem),
+        in_specs=[smem] + [hbm] * 5,
+        out_specs=(hbm, vmem),
         scratch_shapes=[
+            pltpu.VMEM((5, 8, 64, 128), f32),
+            pltpu.VMEM((1, 512), jnp.int32),
             pltpu.VMEM((5, 8, 64, 128), f32),
             pltpu.VMEM((64, 512), jnp.int32),
             pltpu.VMEM((64, 512), f32),
@@ -490,28 +515,25 @@
             pltpu.VMEM((128, 1024), f32),
             pltpu.VMEM((128, 1024), f32),
             dma((4,)),
+            dma((8,)),
             dma((6,)),
             dma((6,)),
-            dma((15,)),
-            dma((15,)),
-            dma((31,)),
-            dma((31,)),
-            dma((15,)),
-            dma((15,)),
-            dma((15,)),
-            dma((15,)),
+            dma((4,)),
+            dma((4,)),
         ],
-        compiler_params=pltpu.CompilerParams(collective_id=0, has_side_effects=True),
+        compiler_params=pltpu.CompilerParams(
+            collective_id=0, has_side_effects=True, vmem_limit_bytes=24 << 20
+        ),
         name="step",
     )(
         panel_counts,
-        panel_cells.reshape(1, panel_cells.shape[0]),
-        conserved,
-        time_bins.T,
-        amplitudes.T,
-        jnp.asarray(filter_rows()),
-    )
-    return (section, signal.reshape(2, OBSERVERS).T)
+        in_hbm(panel_cells.reshape(1, panel_cells.shape[0])),
+        in_hbm(conserved),
+        in_hbm(time_bins.T),
+        in_hbm(amplitudes.T),
+        in_hbm(jnp.asarray(filter_rows())),
+    )
+    return (section, signal.T)
 
 
 def solution(mesh):

time: 49.8 us -> 42.1 us (0.85)
  Pallas kernels: 43.3 us -> 39 us
  local copies, waits for them, and re-layouts: 3.68 us -> 1.62 us
  other arithmetic: 1.3 us -> 0 us
    pallas_call x1, Pallas kernels: 43.3 us -> 39 us  [on_device(): pl.pallas_call(step_kernel, out_shape=(pltpu.VMEM(conserved.shape, f32),...]
    pallas_call x1 -> x0, other arithmetic: 1.3 us -> none  [on_device(): pl.pallas_call(step_kernel, out_shape=(jax.ShapeDtypeStruct(conserved.sha...]
    unnamed x1 -> x2, local copies, waits for them, and re-layouts: 2.52 us -> 1.62 us
    reshape x1 -> x0, local copies, waits for them, and re-layouts: 0.64 us -> none  [on_device(): return (section, signal.reshape(2, OBSERVERS).T)]
    pallas_call x1 -> x0, local copies, waits for them, and re-layouts: 0.51 us -> none  [on_device(): pl.pallas_call(step_kernel, out_shape=(jax.ShapeDtypeStruct(conserved.sha...]
where the time goes in v3:
time: 42.1 us; the launch traced here: 41.9 us
  Pallas kernels  39 us (93%)
  local copies, waits for them, and re-layouts  1.62 us (4%)
  between operations  1.28 us (3%)
    pallas_call x1, Pallas kernels, on_device(): pl.pallas_call(step_kernel, out_shape=(pltpu.VMEM(conserved.shape, f32),...  39 us
    unnamed x2, local copies, waits for them, and re-layouts  1.62 us

profile of v3, /device:TPU:1, one launch (start us, length us, event | category | flops | bytes accessed | tf_op | source)
XLA Modules:
  0.0 41.9 jit_solution(16413605614565512653)
XLA Ops:
  1.3 39.0 %step.1 = (f32[5,8,64,128]{3,2,1,0:T(8,128)S(1)}, f32[2,64]{1,0:T(2,128)S(1)}) custom-call(s32[1]{0:T(128)S(6)} %copy.11.count, s32[1,512]{1,0:T(1,128)} %bitcast.7, f32[5,8,64,128]{3,2,1,0:T(8,128)} %q_hbm.1, s32[64,512]{1,0:T(8,128)} %bitcast.5, f32[64,512]{1,0:T(8,128)} %bitcast.6, f32[8,8,1024]{2,1,0:T(8,128)} %constant.2.clone.h_hbm), custom_call_target="tpu_custom_call" | custom-call | tf_op jit(solution)/shard_map/step/pallas_call | solution.py:486
  40.3 1.1 %copy.10 = f32[5,8,64,128]{3,2,1,0:T(8,128)} copy(f32[5,8,64,128]{3,2,1,0:T(8,128)S(1)} %get-tuple-element.6) | data formatting | bytes 2621440
  41.4 0.6 %copy.12 = f32[64,2]{0,1:T(2,128)} copy(f32[64,2]{0,1:T(2,128)S(1)} %bitcast.4) | data formatting | bytes 1024

commit v4 on v3

--- a/solution.py
+++ b/solution.py
@@ -68,11 +68,13 @@
     amp,
     h,
     axial,
+    relay,
     swirl,
     excess,
     edge_out,
     edge_in,
     inner,
+    turned,
     lines_out,
     lines_in,
     smooth_out,
@@ -180,6 +182,15 @@
             edge_out[0, f, r] = swirl[f, :, 8 + r, :]
             edge_out[1, f, r] = swirl[f, :, 70 + r, :]
 
+    def turn_axial(f, carry):
+        for a in range(4):
+            tile = jnp.concatenate([axial[2 * a + 2, f], axial[2 * a + 3, f]], axis=0)
+            inner[a + 1, f] = tile.T[:8]
+        return carry
+
+    lax.fori_loop(0, 5, turn_axial, 0)
+
+
     @pl.when(ax == 0)
     def _():
         inner[0] = jnp.zeros_like(inner[0])
@@ -238,7 +249,7 @@
             sums[:, pl.ds(i * 8 + k, 1), :] = jnp.concatenate(halves, axis=1).reshape(16, 1, 128)
         return carry
 
-    lax.fori_loop(0, 2, group, 0)
+    lax.fori_loop(0, 4, group, 0)
 
     pl.semaphore_wait(barrier, n_ax - 1 + n_az - 1)
     below, above = axis_ring(n_ax, ax, n_ax - 1), axis_ring(n_ax, ax, 1)
@@ -267,26 +278,18 @@
         above,
         az,
     )
+    @pl.when(ax > 0)
+    def _():
+        inner_down.start()
+
+    @pl.when(ax < n_ax - 1)
+    def _():
+        inner_up.start()
+
     edge_low.start()
     edge_high.start()
-    def turn_axial(f, carry):
-        for a in range(4):
-            tile = jnp.concatenate([axial[2 * a + 2, f], axial[2 * a + 3, f]], axis=0)
-            inner[a + 1, f] = tile.T[:8]
-        return carry
-
-    lax.fori_loop(0, 5, turn_axial, 0)
-
-
-    @pl.when(ax > 0)
-    def _():
-        inner_down.start()
-
-    @pl.when(ax < n_ax - 1)
-    def _():
-        inner_up.start()
-
-    @pl.when(ax > 0)
+
+    @pl.when(jnp.logical_and(ax > 0, ax != n_ax // 2))
     def _():
         halo_down.start()
 
@@ -294,7 +297,6 @@
     def _():
         halo_up.start()
 
-    lax.fori_loop(2, 4, group, 0)
     for r in range(1, n_az):
         peer = axis_ring(n_az, az, r)
         remote(sums.at[peer], sums_in.at[r - 1], bulk_send.at[0], bulk_recv.at[0], ax, peer).start()
@@ -304,55 +306,44 @@
 
     loads[3].wait()
     first = h[...]
-    for k in range(16):
-        g = first if k == 0 else pltpu.roll(first, 8 * k, 1)
-        hi = g.astype(jnp.bfloat16).astype(jnp.float32)
-        g_hi[8 * k : 8 * k + 8] = hi
-        g_lo[8 * k : 8 * k + 8] = g - hi
-
-    edge_low.wait_recv()
-    edge_high.wait_recv()
-    for f in range(5):
-        for r in range(2):
-            swirl[f, :, 6 + r, :] = edge_in[0, f, r]
-            swirl[f, :, 72 + r, :] = edge_in[1, f, r]
-
-    def around(p, carry):
-        for f in range(5):
-            raw[f, p] = raw[f, p] + swirl_gain * (
-                8.0 * (swirl[f, p, 9:73, :] - swirl[f, p, 7:71, :])
-                - (swirl[f, p, 10:74, :] - swirl[f, p, 6:70, :])
-            )
-        return carry
-
-    lax.fori_loop(0, 8, around, 0)
-
-    @pl.when(ax < n_ax - 1)
-    def _():
-        inner_down.wait_recv()
-
-    @pl.when(ax > 0)
-    def _():
-        inner_up.wait_recv()
-
-    upper = lane >= 64
+    for k in range(0, 128, 16):
+        g = jnp.concatenate(
+            [first if k == 0 else pltpu.roll(first, k, 1), pltpu.roll(first, k + 8, 1)], axis=0
+        )
+        g_hi[k : k + 16], g_lo[k : k + 16] = pieces_of(g, 2)
+
     for d in range(n_az):
-        lines_out[d, 8:16, :] = jnp.zeros((8, 128), jnp.float32)
-    lines_out = lines_out
+        lines_out[d, 16:24, :] = jnp.zeros((8, 128), jnp.float32)
 
     def turn_lines(f, carry):
         for a in range(4):
             tile = jnp.concatenate([raw[f, 2 * a], raw[f, 2 * a + 1]], axis=0)
+            turned[f, a] = tile.T[:8]
+            tile = jnp.concatenate([swirl[f, 2 * a, 8:72, :], swirl[f, 2 * a + 1, 8:72, :]], axis=0)
+            lines_out[
+                pl.ds((a // 2) * 8, 8), pl.ds(10 + f * 2 + a % 2, 1), :
+            ] = tile.T[:8].reshape(8, 1, 128)
+        return carry
+
+    lax.fori_loop(0, 5, turn_lines, 0)
+    @pl.when(ax < n_ax - 1)
+    def _():
+        inner_down.wait_recv()
+
+    @pl.when(ax > 0)
+    def _():
+        inner_up.wait_recv()
+
+    upper = lane >= 64
+    for f in range(5):
+        for a in range(4):
             before, now, after = inner[a, f], inner[a + 1, f], inner[a + 2, f]
             next_1 = pltpu.roll(jnp.where(upper, now, after), 64, 1)
             last_1 = pltpu.roll(jnp.where(upper, before, now), 64, 1)
-            line = tile.T[:8] + axial_gain * (8.0 * (next_1 - last_1) - (after - before))
-            lines_out[
-                pl.ds((a // 2) * 8, 8), pl.ds(f * 2 + a % 2, 1), :
-            ] = line.reshape(8, 1, 128)
-        return carry
-
-    lax.fori_loop(0, 5, turn_lines, 0)
+            line = turned[f, a] + axial_gain * (8.0 * (next_1 - last_1) - (after - before))
+            at = (a // 2) * 8
+            row = f * 2 + a % 2
+            lines_out[at : at + 8, row : row + 1, :] = line.reshape(8, 1, 128)
     for r in range(1, n_az):
         peer = axis_ring(n_az, az, r)
         remote(
@@ -364,14 +355,80 @@
     )
 
     lines_in[az] = lines_out[az]
+    middle = n_ax // 2
+    quarters = [pl.ds(16 * k, 16) for k in range(4)]
+    pair_up, pair_down = pl.ds(8, 2), pl.ds(2, 2)
+    land_up, land_down = pl.ds(0, 2), pl.ds(10, 2)
+    routes = []
+    for k, (by_up, by_down) in enumerate(((n_ax - 1, 0), (middle + 1, middle - 2), (n_ax - 2, 1))):
+        rows_k = quarters[k + 1]
+        for source, land, start_ax, by, end_ax, lane_of in (
+            (pair_up, land_up, middle - 1, by_up, middle, 5),
+            (pair_down, land_down, middle, by_down, middle - 1, 4),
+        ):
+            leg = remote(
+                axial.at[source, :, rows_k, :],
+                relay,
+                near_send.at[lane_of],
+                near_recv.at[6],
+                by,
+                az,
+            )
+            forward = remote(
+                relay,
+                axial.at[land, :, rows_k, :],
+                near_send.at[6],
+                near_recv.at[lane_of],
+                end_ax,
+                az,
+            )
+            routes.append((start_ax, by, leg, forward))
+    up_direct = remote(
+        axial.at[pair_up, :, quarters[0], :],
+        axial.at[land_up, :, quarters[0], :],
+        near_send.at[5],
+        near_recv.at[5],
+        middle,
+        az,
+    )
+    down_direct = remote(
+        axial.at[pair_down, :, quarters[0], :],
+        axial.at[land_down, :, quarters[0], :],
+        near_send.at[4],
+        near_recv.at[4],
+        middle - 1,
+        az,
+    )
+    for begins, _, leg, _ in routes:
+
+        @pl.when(ax == begins)
+        def _():
+            leg.start()
+
+    edge_low.wait_recv()
+    edge_high.wait_recv()
+    for f in range(5):
+        for r in range(2):
+            swirl[f, :, 6 + r, :] = edge_in[0, f, r]
+            swirl[f, :, 72 + r, :] = edge_in[1, f, r]
+
+    def around(p, carry):
+        for f in range(5):
+            raw[f, p] = raw[f, p] + swirl_gain * (
+                8.0 * (swirl[f, p, 9:73, :] - swirl[f, p, 7:71, :])
+                - (swirl[f, p, 10:74, :] - swirl[f, p, 6:70, :])
+            )
+        return carry
+
+    lax.fori_loop(0, 8, around, 0)
 
     all_sums.wait_recv()
     total = sums[az]
     for r in range(1, n_az):
         total = total + sums_in[r - 1]
-    turned = total.T
+    flipped = total.T
     rows[...] = jnp.concatenate(
-        [turned[(top * 2 + e) * 32 : (top * 2 + e) * 32 + 32] for e in range(2) for top in range(2)],
+        [flipped[(top * 2 + e) * 32 : (top * 2 + e) * 32 + 32] for e in range(2) for top in range(2)],
         axis=1,
     ).reshape(n_ax, 1, 128)
     for r in range(1, n_ax):
@@ -381,28 +438,55 @@
         rows.at[pl.ds(0, 31)], rows_in, bulk_send.at[2], bulk_recv.at[2], above, az
     )
 
-    @pl.when(ax == n_ax // 2 - 1)
-    def _():
-        halo_up.start()
+    for begins, direct in ((middle - 1, up_direct), (middle, down_direct)):
+
+        @pl.when(ax == begins)
+        def _():
+            direct.start()
 
     all_lines.wait_recv()
+
+    def relay_on(some):
+        for _, by, leg, forward in some:
+
+            @pl.when(ax == by)
+            def _():
+                leg.wait_recv()
+                forward.start()
+
+    relay_on(routes[:2])
     low, high = [], []
     for s in range(0, n_az, 2):
         one, two = lines_in[s], lines_in[s + 1]
         low.append(jnp.where(upper, pltpu.roll(two, 64, 1), one))
         high.append(jnp.where(upper, two, pltpu.roll(one, 64, 1)))
+    cycle = lax.rem(az, CYCLES).astype(jnp.float32) + 0.5
+    gain = jnp.full((1, 128), -time_step / 12.0 / dtheta, jnp.float32) / cycle
+    gain = gain[:, :1]
+
+    def completed(both):
+        change = 8.0 * (
+            pltpu.roll(both, AZIMUTH - 1, 1) - pltpu.roll(both, 1, 1)
+        ) - (pltpu.roll(both, AZIMUTH - 2, 1) - pltpu.roll(both, 2, 1))
+        return both[:16] + gain * pltpu.roll(change, 14, 0)[:16]
+
     x = jnp.concatenate(
-        [jnp.concatenate(low, axis=1), jnp.concatenate(high, axis=1)], axis=0
-    )
-    turns = jnp.concatenate(
-        [
-            x if a == 0 else jnp.concatenate([x[:, 128 * a :], x[:, : 128 * a]], axis=1)
-            for a in range(8)
-        ],
-        axis=0,
-    )
-    x_hi, x_lo = pieces_of(turns, 2)
-    k_hi, k_lo = g_hi[...].astype(jnp.bfloat16), g_lo[...].astype(jnp.bfloat16)
+        [completed(jnp.concatenate(low, axis=1)), completed(jnp.concatenate(high, axis=1))], axis=0
+    )
+
+    def turns(part):
+        return jnp.concatenate(
+            [
+                part
+                if a == 0
+                else jnp.concatenate([part[:, 128 * a :], part[:, : 128 * a]], axis=1)
+                for a in range(8)
+            ],
+            axis=0,
+        )
+
+    x_hi, x_lo = [turns(part) for part in pieces_of(x, 2)]
+    k_hi, k_lo = g_hi[...], g_lo[...]
     y = dot_t(x_hi, k_hi) + (dot_t(x_lo, k_hi) + dot_t(x_hi, k_lo))
     for a in range(8):
         one, two = y[32 * a : 32 * a + 16], y[32 * a + 16 : 32 * a + 32]
@@ -417,6 +501,7 @@
         smooth_out.at[most], smooth_in.at[most], bulk_send.at[3], bulk_recv.at[3], ax, right_az
     )
     smooth_in[az] = smooth_out[az]
+    relay_on(routes[2:])
     @pl.when(ax < n_ax - 1)
     def _():
         halo_down.wait_recv()
@@ -472,6 +557,22 @@
         inner_up.wait_send()
         halo_up.wait_send()
 
+    for _, by, _, forward in routes:
+
+        @pl.when(ax == by)
+        def _():
+            forward.wait_send()
+
+
+def leave_kernel(raw, sig, section_ref, sig_ref, sem):
+    copies = [
+        pltpu.make_async_copy(raw.at[f], section_ref.at[f], sem.at[f]) for f in range(5)
+    ] + [pltpu.make_async_copy(sig, sig_ref, sem.at[5])]
+    for copy in copies:
+        copy.start()
+    for copy in copies:
+        copy.wait()
+
 
 def on_device(conserved, panel_cells, panel_counts, time_bins, amplitudes):
     f32 = jnp.float32
@@ -483,11 +584,14 @@
     def in_hbm(value):
         return pltpu.with_memory_space_constraint(value, pltpu.HBM)
 
+    def in_vmem(value):
+        return pltpu.with_memory_space_constraint(value, pltpu.VMEM)
+
     section, signal = pl.pallas_call(
         step_kernel,
         out_shape=(
             pltpu.VMEM(conserved.shape, f32),
-            jax.ShapeDtypeStruct((2, 64), f32),
+            pltpu.VMEM((2, 64), f32),
         ),
         in_specs=[smem] + [hbm] * 5,
         out_specs=(hbm, vmem),
@@ -499,25 +603,27 @@
             pltpu.VMEM((64, 512), f32),
             pltpu.VMEM((8, 1024), f32),
             pltpu.VMEM((12, 5, 64, 128), f32),
+            pltpu.VMEM((2, 5, 16, 128), f32),
             pltpu.VMEM((5, 8, 80, 128), f32),
             pltpu.VMEM((512, 128), f32),
             pltpu.VMEM((2, 5, 2, 8, 128), f32),
             pltpu.VMEM((2, 5, 2, 8, 128), f32),
             pltpu.VMEM((6, 5, 8, 128), f32),
-            pltpu.VMEM((16, 16, 128), f32),
-            pltpu.VMEM((16, 16, 128), f32),
+            pltpu.VMEM((5, 4, 8, 128), f32),
+            pltpu.VMEM((16, 24, 128), f32),
+            pltpu.VMEM((16, 24, 128), f32),
             pltpu.VMEM((16, 16, 128), f32),
             pltpu.VMEM((16, 16, 128), f32),
             pltpu.VMEM((16, 32, 128), f32),
             pltpu.VMEM((15, 32, 128), f32),
             pltpu.VMEM((32, 1, 128), f32),
             pltpu.VMEM((31, 1, 128), f32),
-            pltpu.VMEM((128, 1024), f32),
-            pltpu.VMEM((128, 1024), f32),
+            pltpu.VMEM((128, 1024), jnp.bfloat16),
+            pltpu.VMEM((128, 1024), jnp.bfloat16),
             dma((4,)),
             dma((8,)),
-            dma((6,)),
-            dma((6,)),
+            dma((7,)),
+            dma((7,)),
             dma((4,)),
             dma((4,)),
         ],
@@ -533,6 +639,18 @@
         in_hbm(amplitudes.T),
         in_hbm(jnp.asarray(filter_rows())),
     )
+    section, signal = pl.pallas_call(
+        leave_kernel,
+        out_shape=(
+            jax.ShapeDtypeStruct(conserved.shape, f32),
+            jax.ShapeDtypeStruct((2, 64), f32),
+        ),
+        in_specs=[hbm, hbm],
+        out_specs=(hbm, hbm),
+        scratch_shapes=[dma((6,))],
+        compiler_params=pltpu.CompilerParams(vmem_limit_bytes=8 << 20),
+        name="leave",
+    )(in_vmem(section), in_vmem(signal))
     return (section, signal.T)
 
 

time: 42.1 us -> 37.4 us (0.89)
  Pallas kernels: 39 us -> 36 us
  local copies, waits for them, and re-layouts: 1.62 us -> 0 us
    pallas_call x1, Pallas kernels: 39 us -> 34.9 us  [on_device(): pl.pallas_call(step_kernel, out_shape=(pltpu.VMEM(conserved.shape, f32),...]
    unnamed x2 -> x0, local copies, waits for them, and re-layouts: 1.62 us -> none
    pallas_call x0 -> x1, Pallas kernels: none -> 1.1 us  [on_device(): pl.pallas_call(leave_kernel, out_shape=(jax.ShapeDtypeStruct(conserved.sh...]
where the time goes in v4:
time: 37.4 us; the launch traced here: 37.2 us
  Pallas kernels  36 us (96%)
  between operations  1.28 us (3%)
    pallas_call x1, Pallas kernels, on_device(): pl.pallas_call(step_kernel, out_shape=(pltpu.VMEM(conserved.shape, f32),...  34.9 us
    pallas_call x1, Pallas kernels, on_device(): pl.pallas_call(leave_kernel, out_shape=(jax.ShapeDtypeStruct(conserved.sh...  1.1 us

profile of v4, /device:TPU:1, one launch (start us, length us, event | category | flops | bytes accessed | tf_op | source)
XLA Modules:
  0.0 37.2 jit_solution(6561290596097056735)
XLA Ops:
  1.3 34.9 %step.1 = (f32[5,8,64,128]{3,2,1,0:T(8,128)S(1)}, f32[2,64]{1,0:T(2,128)S(1)}) custom-call(s32[1]{0:T(128)S(6)} %copy.8.count, s32[1,512]{1,0:T(1,128)} %bitcast.6, f32[5,8,64,128]{3,2,1,0:T(8,128)} %q_hbm.1, s32[64,512]{1,0:T(8,128)} %bitcast.4, f32[64,512]{1,0:T(8,128)} %bitcast.5, f32[8,8,1024]{2,1,0:T(8,128)} %constant.2.clone.h_hbm), custom_call_target="tpu_custom_call" | custom-call | tf_op jit(solution)/shard_map/step/pallas_call | solution.py:590
  36.1 1.1 %leave.1 = (f32[5,8,64,128]{3,2,1,0:T(8,128)}, f32[2,64]{1,0:T(2,128)}) custom-call(f32[5,8,64,128]{3,2,1,0:T(8,128)S(1)} %get-tuple-element.6.raw, f32[2,64]{1,0:T(2,128)S(1)} %get-tuple-element.7.sig), custom_call_target="tpu_custom_call" | custom-call | tf_op jit(solution)/shard_map/leave/pallas_call | solution.py:642

commit v5 on v4

--- a/solution.py
+++ b/solution.py
@@ -119,6 +119,8 @@
         plane_load(p).start()
     for copy in loads:
         copy.start()
+    for d in range(n_az):
+        lines_in[d, 16:24, :] = jnp.zeros((8, 128), jnp.float32)
     barrier = pltpu.get_barrier_semaphore()
     for k in range(1, n_ax):
         r = n_ax // 2 + (k // 2 if k % 2 == 0 else -(k // 2))
@@ -344,59 +346,43 @@
             at = (a // 2) * 8
             row = f * 2 + a % 2
             lines_out[at : at + 8, row : row + 1, :] = line.reshape(8, 1, 128)
+    filled = pl.ds(0, 20)
     for r in range(1, n_az):
         peer = axis_ring(n_az, az, r)
         remote(
-            lines_out.at[peer], lines_in.at[az], bulk_send.at[1], bulk_recv.at[1], ax, peer
+            lines_out.at[peer, filled], lines_in.at[az, filled], bulk_send.at[1], bulk_recv.at[1], ax, peer
         ).start()
     most = pl.ds(0, 15)
     all_lines = remote(
-        lines_out.at[most], lines_in.at[most], bulk_send.at[1], bulk_recv.at[1], ax, right_az
+        lines_out.at[most, filled], lines_in.at[most, filled], bulk_send.at[1], bulk_recv.at[1], ax, right_az
     )
 
     lines_in[az] = lines_out[az]
     middle = n_ax // 2
-    quarters = [pl.ds(16 * k, 16) for k in range(4)]
-    pair_up, pair_down = pl.ds(8, 2), pl.ds(2, 2)
-    land_up, land_down = pl.ds(0, 2), pl.ds(10, 2)
+    pair_up, land_up = pl.ds(8, 2), pl.ds(0, 2)
     routes = []
-    for k, (by_up, by_down) in enumerate(((n_ax - 1, 0), (middle + 1, middle - 2), (n_ax - 2, 1))):
-        rows_k = quarters[k + 1]
-        for source, land, start_ax, by, end_ax, lane_of in (
-            (pair_up, land_up, middle - 1, by_up, middle, 5),
-            (pair_down, land_down, middle, by_down, middle - 1, 4),
-        ):
-            leg = remote(
-                axial.at[source, :, rows_k, :],
-                relay,
-                near_send.at[lane_of],
-                near_recv.at[6],
-                by,
-                az,
-            )
-            forward = remote(
-                relay,
-                axial.at[land, :, rows_k, :],
-                near_send.at[6],
-                near_recv.at[lane_of],
-                end_ax,
-                az,
-            )
-            routes.append((start_ax, by, leg, forward))
+    for by, start, size, place, slot in (
+        (n_ax - 1, 8, 24, 0, 6),
+        (n_ax - 1, 32, 16, 24, 7),
+        (middle + 1, 48, 8, 0, 6),
+        (n_ax - 2, 56, 8, 0, 6),
+    ):
+        share = pl.ds(start, size)
+        stop = relay.at[:, :, pl.ds(place, size), :]
+        leg = remote(
+            axial.at[pair_up, :, share, :], stop, near_send.at[5], near_recv.at[slot], by, az
+        )
+        forward = remote(
+            stop, axial.at[land_up, :, share, :], near_send.at[slot], near_recv.at[5], middle, az
+        )
+        routes.append((middle - 1, by, leg, forward))
+    share = pl.ds(0, 8)
     up_direct = remote(
-        axial.at[pair_up, :, quarters[0], :],
-        axial.at[land_up, :, quarters[0], :],
+        axial.at[pair_up, :, share, :],
+        axial.at[land_up, :, share, :],
         near_send.at[5],
         near_recv.at[5],
         middle,
-        az,
-    )
-    down_direct = remote(
-        axial.at[pair_down, :, quarters[0], :],
-        axial.at[land_down, :, quarters[0], :],
-        near_send.at[4],
-        near_recv.at[4],
-        middle - 1,
         az,
     )
     for begins, _, leg, _ in routes:
@@ -438,13 +424,13 @@
         rows.at[pl.ds(0, 31)], rows_in, bulk_send.at[2], bulk_recv.at[2], above, az
     )
 
-    for begins, direct in ((middle - 1, up_direct), (middle, down_direct)):
-
-        @pl.when(ax == begins)
-        def _():
-            direct.start()
-
-    all_lines.wait_recv()
+    @pl.when(ax == middle - 1)
+    def _():
+        up_direct.start()
+
+    @pl.when(ax == middle)
+    def _():
+        halo_down.start()
 
     def relay_on(some):
         for _, by, leg, forward in some:
@@ -454,7 +440,10 @@
                 leg.wait_recv()
                 forward.start()
 
-    relay_on(routes[:2])
+    relay_on(routes[:1])
+    all_lines.wait_recv()
+    relay_on(routes[1:2])
+
     low, high = [], []
     for s in range(0, n_az, 2):
         one, two = lines_in[s], lines_in[s + 1]
@@ -492,13 +481,14 @@
         one, two = y[32 * a : 32 * a + 16], y[32 * a + 16 : 32 * a + 32]
         smooth_out[2 * a] = jnp.where(upper, pltpu.roll(two, 64, 1), one)
         smooth_out[2 * a + 1] = jnp.where(upper, two, pltpu.roll(one, 64, 1))
+    used = pl.ds(0, 10)
     for r in range(1, n_az):
         peer = axis_ring(n_az, az, r)
         remote(
-            smooth_out.at[peer], smooth_in.at[az], bulk_send.at[3], bulk_recv.at[3], ax, peer
+            smooth_out.at[peer, used], smooth_in.at[az, used], bulk_send.at[3], bulk_recv.at[3], ax, peer
         ).start()
     all_smooth = remote(
-        smooth_out.at[most], smooth_in.at[most], bulk_send.at[3], bulk_recv.at[3], ax, right_az
+        smooth_out.at[most, used], smooth_in.at[most, used], bulk_send.at[3], bulk_recv.at[3], ax, right_az
     )
     smooth_in[az] = smooth_out[az]
     relay_on(routes[2:])
@@ -603,7 +593,7 @@
             pltpu.VMEM((64, 512), f32),
             pltpu.VMEM((8, 1024), f32),
             pltpu.VMEM((12, 5, 64, 128), f32),
-            pltpu.VMEM((2, 5, 16, 128), f32),
+            pltpu.VMEM((2, 5, 40, 128), f32),
             pltpu.VMEM((5, 8, 80, 128), f32),
             pltpu.VMEM((512, 128), f32),
             pltpu.VMEM((2, 5, 2, 8, 128), f32),
@@ -622,8 +612,8 @@
             pltpu.VMEM((128, 1024), jnp.bfloat16),
             dma((4,)),
             dma((8,)),
-            dma((7,)),
-            dma((7,)),
+            dma((8,)),
+            dma((8,)),
             dma((4,)),
             dma((4,)),
         ],

time: 37.4 us -> 36.3 us (0.971)
  Pallas kernels: 36 us -> 34.8 us
    pallas_call x1, Pallas kernels: 34.9 us -> 33.7 us  [on_device(): pl.pallas_call(step_kernel, out_shape=(pltpu.VMEM(conserved.shape, f32),...]
where the time goes in v5:
time: 36.3 us; the launch traced here: 36.1 us
  Pallas kernels  34.8 us (96%)
  between operations  1.28 us (4%)
    pallas_call x1, Pallas kernels, on_device(): pl.pallas_call(step_kernel, out_shape=(pltpu.VMEM(conserved.shape, f32),...  33.7 us
    pallas_call x1, Pallas kernels, on_device(): pl.pallas_call(leave_kernel, out_shape=(jax.ShapeDtypeStruct(conserved.sh...  1.1 us

profile of v5, /device:TPU:1, one launch (start us, length us, event | category | flops | bytes accessed | tf_op | source)
XLA Modules:
  0.0 36.1 jit_solution(11840381722250138006)
XLA Ops:
  1.3 33.7 %step.1 = (f32[5,8,64,128]{3,2,1,0:T(8,128)S(1)}, f32[2,64]{1,0:T(2,128)S(1)}) custom-call(s32[1]{0:T(128)S(6)} %copy.8.count, s32[1,512]{1,0:T(1,128)} %bitcast.6, f32[5,8,64,128]{3,2,1,0:T(8,128)} %q_hbm.1, s32[64,512]{1,0:T(8,128)} %bitcast.4, f32[64,512]{1,0:T(8,128)} %bitcast.5, f32[8,8,1024]{2,1,0:T(8,128)} %constant.2.clone.h_hbm), custom_call_target="tpu_custom_call" | custom-call | tf_op jit(solution)/shard_map/step/pallas_call | solution.py:580
  35.0 1.1 %leave.1 = (f32[5,8,64,128]{3,2,1,0:T(8,128)}, f32[2,64]{1,0:T(2,128)}) custom-call(f32[5,8,64,128]{3,2,1,0:T(8,128)S(1)} %get-tuple-element.6.raw, f32[2,64]{1,0:T(2,128)S(1)} %get-tuple-element.7.sig), custom_call_target="tpu_custom_call" | custom-call | tf_op jit(solution)/shard_map/leave/pallas_call | solution.py:632

commit v6 on v5

--- a/solution.py
+++ b/solution.py
@@ -81,6 +81,7 @@
     smooth_in,
     sums,
     sums_in,
+    core_in,
     rows,
     rows_in,
     g_hi,
@@ -232,7 +233,7 @@
             b = bins[at, :]
             contrib = sampled * amp[at, :]
             main = contrib.astype(jnp.bfloat16).astype(jnp.float32)
-            owner = ((b >> 1) & 15).astype(jnp.float32)
+            owner = (((b >> 2) & 7) | ((b & 2) << 2)).astype(jnp.float32)
             rest = (((b & 1) << 5) | (b >> 5)).astype(jnp.float32)
             ready.append((main, contrib - main, owner, rest))
         for k in range(8):
@@ -299,12 +300,12 @@
     def _():
         halo_up.start()
 
-    for r in range(1, n_az):
-        peer = axis_ring(n_az, az, r)
-        remote(sums.at[peer], sums_in.at[r - 1], bulk_send.at[0], bulk_recv.at[0], ax, peer).start()
-    all_sums = remote(
-        sums.at[pl.ds(0, 15)], sums_in, bulk_send.at[0], bulk_recv.at[0], ax, right_az
-    )
+    core, chip = lax.rem(az, 2), az // 2
+    mine, others = pl.ds(core * 8, 8), pl.ds((1 - core) * 8, 8)
+    to_core = remote(
+        sums.at[others], core_in, near_send.at[8], near_recv.at[8], ax, az + 1 - 2 * core
+    )
+    to_core.start()
 
     loads[3].wait()
     first = h[...]
@@ -328,6 +329,22 @@
         return carry
 
     lax.fori_loop(0, 5, turn_lines, 0)
+    to_core.wait_recv()
+    sums[mine] = sums[mine] + core_in[...]
+    for r in range(1, 8):
+        other = axis_ring(8, chip, r)
+        remote(
+            sums.at[core * 8 + other],
+            sums_in.at[r - 1],
+            bulk_send.at[0],
+            bulk_recv.at[0],
+            ax,
+            other * 2 + core,
+        ).start()
+    all_sums = remote(
+        sums.at[pl.ds(0, 7)], sums_in, bulk_send.at[0], bulk_recv.at[0], ax, right_az
+    )
+
     @pl.when(ax < n_ax - 1)
     def _():
         inner_down.wait_recv()
@@ -409,8 +426,8 @@
     lax.fori_loop(0, 8, around, 0)
 
     all_sums.wait_recv()
-    total = sums[az]
-    for r in range(1, n_az):
+    total = sums[core * 8 + chip]
+    for r in range(1, 8):
         total = total + sums_in[r - 1]
     flipped = total.T
     rows[...] = jnp.concatenate(
@@ -454,10 +471,11 @@
     gain = gain[:, :1]
 
     def completed(both):
+        swirls = both[8:24]
         change = 8.0 * (
-            pltpu.roll(both, AZIMUTH - 1, 1) - pltpu.roll(both, 1, 1)
-        ) - (pltpu.roll(both, AZIMUTH - 2, 1) - pltpu.roll(both, 2, 1))
-        return both[:16] + gain * pltpu.roll(change, 14, 0)[:16]
+            pltpu.roll(swirls, AZIMUTH - 1, 1) - pltpu.roll(swirls, 1, 1)
+        ) - (pltpu.roll(swirls, AZIMUTH - 2, 1) - pltpu.roll(swirls, 2, 1))
+        return both[:16] + gain * pltpu.roll(change, 14, 0)
 
     x = jnp.concatenate(
         [completed(jnp.concatenate(low, axis=1)), completed(jnp.concatenate(high, axis=1))], axis=0
@@ -534,7 +552,7 @@
     sig_ref[...] = jnp.concatenate([total[:, :64], total[:, 64:]], axis=0)
 
     section_copy.wait()
-    for copy in (edge_low, edge_high, all_sums, all_lines, all_rows, all_smooth):
+    for copy in (edge_low, edge_high, to_core, all_sums, all_lines, all_rows, all_smooth):
         copy.wait_send()
 
     @pl.when(ax > 0)
@@ -605,15 +623,16 @@
             pltpu.VMEM((16, 16, 128), f32),
             pltpu.VMEM((16, 16, 128), f32),
             pltpu.VMEM((16, 32, 128), f32),
-            pltpu.VMEM((15, 32, 128), f32),
+            pltpu.VMEM((7, 32, 128), f32),
+            pltpu.VMEM((8, 32, 128), f32),
             pltpu.VMEM((32, 1, 128), f32),
             pltpu.VMEM((31, 1, 128), f32),
             pltpu.VMEM((128, 1024), jnp.bfloat16),
             pltpu.VMEM((128, 1024), jnp.bfloat16),
             dma((4,)),
             dma((8,)),
-            dma((8,)),
-            dma((8,)),
+            dma((9,)),
+            dma((9,)),
             dma((4,)),
             dma((4,)),
         ],

time: 36.3 us -> 35.5 us (0.978)
  Pallas kernels: 34.8 us -> 34.1 us
    pallas_call x1, Pallas kernels: 33.7 us -> 33 us  [on_device(): pl.pallas_call(step_kernel, out_shape=(pltpu.VMEM(conserved.shape, f32),...]
where the time goes in v6:
time: 35.5 us; the launch traced here: 35.3 us
  Pallas kernels  34.1 us (96%)
  between operations  1.28 us (4%)
    pallas_call x1, Pallas kernels, on_device(): pl.pallas_call(step_kernel, out_shape=(pltpu.VMEM(conserved.shape, f32),...  33 us
    pallas_call x1, Pallas kernels, on_device(): pl.pallas_call(leave_kernel, out_shape=(jax.ShapeDtypeStruct(conserved.sh...  1.1 us

profile of v6, /device:TPU:1, one launch (start us, length us, event | category | flops | bytes accessed | tf_op | source)
XLA Modules:
  0.0 35.3 jit_solution(9058357517518381405)
XLA Ops:
  1.3 33.0 %step.1 = (f32[5,8,64,128]{3,2,1,0:T(8,128)S(1)}, f32[2,64]{1,0:T(2,128)S(1)}) custom-call(s32[1]{0:T(128)S(6)} %copy.8.count, s32[1,512]{1,0:T(1,128)} %bitcast.6, f32[5,8,64,128]{3,2,1,0:T(8,128)} %q_hbm.1, s32[64,512]{1,0:T(8,128)} %bitcast.4, f32[64,512]{1,0:T(8,128)} %bitcast.5, f32[8,8,1024]{2,1,0:T(8,128)} %constant.2.clone.h_hbm), custom_call_target="tpu_custom_call" | custom-call | tf_op jit(solution)/shard_map/step/pallas_call | solution.py:598
  34.2 1.1 %leave.1 = (f32[5,8,64,128]{3,2,1,0:T(8,128)}, f32[2,64]{1,0:T(2,128)}) custom-call(f32[5,8,64,128]{3,2,1,0:T(8,128)S(1)} %get-tuple-element.6.raw, f32[2,64]{1,0:T(2,128)S(1)} %get-tuple-element.7.sig), custom_call_target="tpu_custom_call" | custom-call | tf_op jit(solution)/shard_map/leave/pallas_call | solution.py:651

commit v7 on v6

--- a/solution.py
+++ b/solution.py
@@ -379,8 +379,8 @@
     pair_up, land_up = pl.ds(8, 2), pl.ds(0, 2)
     routes = []
     for by, start, size, place, slot in (
-        (n_ax - 1, 8, 24, 0, 6),
-        (n_ax - 1, 32, 16, 24, 7),
+        (n_ax - 1, 16, 24, 0, 6),
+        (n_ax - 1, 40, 8, 24, 7),
         (middle + 1, 48, 8, 0, 6),
         (n_ax - 2, 56, 8, 0, 6),
     ):
@@ -393,7 +393,7 @@
             stop, axial.at[land_up, :, share, :], near_send.at[slot], near_recv.at[5], middle, az
         )
         routes.append((middle - 1, by, leg, forward))
-    share = pl.ds(0, 8)
+    share = pl.ds(0, 16)
     up_direct = remote(
         axial.at[pair_up, :, share, :],
         axial.at[land_up, :, share, :],
@@ -611,7 +611,7 @@
             pltpu.VMEM((64, 512), f32),
             pltpu.VMEM((8, 1024), f32),
             pltpu.VMEM((12, 5, 64, 128), f32),
-            pltpu.VMEM((2, 5, 40, 128), f32),
+            pltpu.VMEM((2, 5, 32, 128), f32),
             pltpu.VMEM((5, 8, 80, 128), f32),
             pltpu.VMEM((512, 128), f32),
             pltpu.VMEM((2, 5, 2, 8, 128), f32),

time: 35.5 us -> 35.5 us (level)
  no operation moved by 1% of the time
where the time goes in v7:
time: 35.5 us; the launch traced here: 35.3 us
  Pallas kernels  34.1 us (96%)
  between operations  1.28 us (4%)
    pallas_call x1, Pallas kernels, on_device(): pl.pallas_call(step_kernel, out_shape=(pltpu.VMEM(conserved.shape, f32),...  33 us
    pallas_call x1, Pallas kernels, on_device(): pl.pallas_call(leave_kernel, out_shape=(jax.ShapeDtypeStruct(conserved.sh...  1.1 us

profile of v7, /device:TPU:1, one launch (start us, length us, event | category | flops | bytes accessed | tf_op | source)
XLA Modules:
  0.0 35.3 jit_solution(18061559093460980982)
XLA Ops:
  1.3 33.0 %step.1 = (f32[5,8,64,128]{3,2,1,0:T(8,128)S(1)}, f32[2,64]{1,0:T(2,128)S(1)}) custom-call(s32[1]{0:T(128)S(6)} %copy.8.count, s32[1,512]{1,0:T(1,128)} %bitcast.6, f32[5,8,64,128]{3,2,1,0:T(8,128)} %q_hbm.1, s32[64,512]{1,0:T(8,128)} %bitcast.4, f32[64,512]{1,0:T(8,128)} %bitcast.5, f32[8,8,1024]{2,1,0:T(8,128)} %constant.2.clone.h_hbm), custom_call_target="tpu_custom_call" | custom-call | tf_op jit(solution)/shard_map/step/pallas_call | solution.py:598
  34.2 1.1 %leave.1 = (f32[5,8,64,128]{3,2,1,0:T(8,128)}, f32[2,64]{1,0:T(2,128)}) custom-call(f32[5,8,64,128]{3,2,1,0:T(8,128)S(1)} %get-tuple-element.6.raw, f32[2,64]{1,0:T(2,128)S(1)} %get-tuple-element.7.sig), custom_call_target="tpu_custom_call" | custom-call | tf_op jit(solution)/shard_map/leave/pallas_call | solution.py:651
